TPU v7x, 32 devices: a whole 2x2x4 slice. The times are simulated.
32 devices in a mesh: groups: 2 (over x), seq: 8 (over z, y), head: 2 (over core).
Axes of the slice: x: 2, y: 2, z: 4, core: 2. Of those that a mesh axis runs over, the one named last changes fastest.
Arguments:
- query_proj: bfloat16 [4096, 2048], P(('groups', 'seq'), 'head'), parts along dimension 0, may hold values from -6 to 6
- key_proj: bfloat16 [4096, 2048], P(('groups', 'seq'), 'head'), parts along dimension 0, may hold values from -6 to 6
- value_proj: bfloat16 [4096, 2048], P(('groups', 'seq'), 'head'), parts along dimension 0, may hold values from -6 to 6
- segment_ids: int32 [4096], P(('groups', 'seq')), parts along dimension 0, may hold values from 0 to 5, never falling along the last dimension, each value on 1 to 682 neighbouring positions
- feature_map: bfloat16 [16, 128, 256], P('head'), may hold values from -0.5 to 0.5
- head_gain: float32 [2048], P('head'), may hold values from 0.1 to 1.9
- residual: bfloat16 [4096, 2048], P(('groups', 'seq', 'head')), parts along dimension 0, may hold values from -6 to 6
- out_weight: bfloat16 [2048, 2048], P('head'), may hold values from -0.125 to 0.125
- norm_gain: float32 [2048], replicated, may hold values from 0.1 to 1.9
- router: bfloat16 [2048, 16], replicated, may hold values from -0.125 to 0.125
- w_gate: bfloat16 [16, 2048, 1024], P(('seq', 'head')), may hold values from -0.125 to 0.125
- w_up: bfloat16 [16, 2048, 1024], P(('seq', 'head')), may hold values from -0.125 to 0.125
- w_down: bfloat16 [16, 1024, 2048], P(('seq', 'head')), may hold values from -0.1875 to 0.1875
- expert_ids: int32 [4096, 8], P(('groups', 'seq', 'head')), parts along dimension 0, may hold values from 0 to 15, all different within a row; in each aligned block of 128 rows (0 to 127, 128 to 255, ...) at most 80 rows name the same one
Outputs:
- hidden: bfloat16 [4096, 2048], P(('groups', 'seq', 'head')), parts along dimension 0
- expert_sum: bfloat16 [4096, 2048], P(('groups', 'seq', 'head')), parts along dimension 0
There are 2 independent parts, one for each index of `groups`. A program takes and returns all parts, laid end to end along the dimension named above; an argument that names none is the same for every part. Nothing has to cross between parts.
Inputs may be any that keep to these rules, and one draw needn't show every extreme that they name: `segment_ids`: segment ids never fall; every segment has 1 to 682 tokens, one exactly 682. `expert_ids`: A token's 8 experts differ. In the 128 rows of one device (aligned blocks of rows) no expert is named more than 80 times, and in some such block some expert is named exactly 80 times.
All inputs are finite; a program needn't handle non-finite values.
Results may differ from a plain program's by a relative error of at most 0.011.
Values may be sent and summed in bfloat16 or wider, within the bound.
A program may use at most 128 MiB of HBM per device.

v0:
```python
import jax
import jax.numpy as jnp
from jax import lax
from jax.sharding import PartitionSpec as P


def carried_in(part, axis, combine, identity):
    place = lax.axis_index(axis)
    gathered = jax.tree.map(lambda a: lax.all_gather(a, axis), part)
    state = jax.tree.map(lambda a, e: jnp.zeros_like(a) + jnp.asarray(e, a.dtype), part, identity)

    def one(hop, state):
        return combine(
            state, jax.tree.map(lambda a: lax.dynamic_index_in_dim(a, hop, 0, False), gathered)
        )

    return lax.fori_loop(0, place, one, state)


def features_of(inputs, feature_map, head_count, head_dim):
    grouped = inputs.reshape(inputs.shape[0], head_count, head_dim)
    projected = jnp.einsum("thd,hdf->thf", grouped, feature_map, preferred_element_type=jnp.float32)
    return (jax.nn.elu(projected) + 1.0).astype(jnp.bfloat16)


def combine_states(earlier, later):
    same_seg = (earlier[0] == later[0]).astype(jnp.float32)
    return (later[0], later[1] + same_seg * earlier[1])


def run_experts(received, w_gate, w_up, w_down):
    gate_pre = jnp.einsum("gecd,edf->gecf", received, w_gate, preferred_element_type=jnp.float32)
    up_pre = jnp.einsum("gecd,edf->gecf", received, w_up, preferred_element_type=jnp.float32)
    activated = (jax.nn.silu(gate_pre) * up_pre).astype(jnp.bfloat16)
    return jnp.einsum(
        "gecf,efd->gecd", activated, w_down, preferred_element_type=jnp.float32
    ).astype(jnp.bfloat16)


def shards(
    query_proj,
    key_proj,
    value_proj,
    segment_ids,
    feature_map,
    head_gain,
    residual,
    out_weight,
    norm_gain,
    router,
    w_gate,
    w_up,
    w_down,
    expert_ids,
):
    token_count = query_proj.shape[0]
    head_count = feature_map.shape[0]
    head_dim = feature_map.shape[1]
    query_feat = features_of(query_proj, feature_map, head_count, head_dim)
    key_feat = features_of(key_proj, feature_map, head_count, head_dim)
    values = value_proj.reshape(token_count, head_count, head_dim)
    last_seg = segment_ids[token_count - 1]
    tail_mask = (segment_ids == last_seg).astype(jnp.bfloat16)
    local_state = jnp.einsum(
        "thf,thd->hfd",
        key_feat * tail_mask[:, None, None],
        values,
        preferred_element_type=jnp.float32,
    )
    identity = (jnp.array(-1, dtype=jnp.int32), jnp.zeros_like(local_state))
    seg_before, state_before = carried_in((last_seg, local_state), "seq", combine_states, identity)
    scores = jnp.einsum("thf,shf->hts", query_feat, key_feat, preferred_element_type=jnp.float32)
    positions = lax.iota(jnp.int32, token_count)
    allowed = (positions[None, :] <= positions[:, None]) & (
        segment_ids[None, :] == segment_ids[:, None]
    )
    block_weights = jnp.where(allowed[None], scores, 0.0).astype(jnp.bfloat16)
    within = jnp.einsum("hts,shd->thd", block_weights, values, preferred_element_type=jnp.float32)
    carried = jnp.einsum(
        "thf,hfd->thd",
        query_feat.astype(jnp.float32),
        state_before,
        precision=lax.Precision.HIGHEST,
    )
    carry_mask = (segment_ids == seg_before).astype(jnp.float32)
    mixed = within + carry_mask[:, None, None] * carried
    scale = lax.rsqrt(jnp.mean(mixed * mixed, axis=2, keepdims=True) + 1e-06)
    attn_heads = (
        (mixed * scale * head_gain.reshape(head_count, head_dim))
        .reshape(token_count, head_count * head_dim)
        .astype(jnp.bfloat16)
    )
    row_count = residual.shape[0]
    attn_rows = lax.all_to_all(attn_heads, "head", split_axis=0, concat_axis=1, tiled=True)
    projected = jnp.dot(
        attn_rows,
        lax.all_gather(out_weight, "head", axis=0, tiled=True),
        preferred_element_type=jnp.float32,
    )
    hidden = (residual.astype(jnp.float32) + projected).astype(jnp.bfloat16)
    hidden_f = hidden.astype(jnp.float32)
    normed = (
        hidden_f
        * lax.rsqrt(jnp.mean(hidden_f * hidden_f, axis=1, keepdims=True) + 1e-05)
        * norm_gain
    ).astype(jnp.bfloat16)
    logits = jnp.dot(normed, router, preferred_element_type=jnp.float32)
    expert_count = router.shape[1]
    top_count = expert_ids.shape[1]
    model_width = normed.shape[1]
    expert_iota = lax.iota(jnp.int32, expert_count)
    picked = expert_ids[:, :, None] == expert_iota[None, None, :]
    chosen = jnp.sum(jnp.where(picked, logits[:, None, :], 0.0), axis=2)
    gates = jax.nn.sigmoid(chosen)
    gate_weights = gates / jnp.sum(gates, axis=1, keepdims=True)
    capacity = row_count * top_count * 5 // (4 * expert_count)
    onehot = picked.reshape(row_count * top_count, expert_count).astype(jnp.int32)
    slots = jnp.sum((jnp.cumsum(onehot, axis=0) - onehot) * onehot, axis=1)
    targets = expert_ids.reshape(-1) * capacity + slots
    slot_iota = lax.iota(jnp.int32, expert_count * capacity)
    dispatch = jnp.any(
        targets.reshape(row_count, top_count)[:, :, None] == slot_iota[None, None, :], axis=1
    ).astype(jnp.bfloat16)
    send_rows = jnp.einsum(
        "rs,rd->sd", dispatch, normed, preferred_element_type=jnp.float32
    ).astype(jnp.bfloat16)
    exp_dev = w_gate.shape[0]
    seq_count = lax.axis_size("seq")
    head_devs = lax.axis_size("head")
    arrived = lax.all_to_all(
        send_rows.reshape(expert_count, capacity, model_width),
        ("seq", "head"),
        split_axis=0,
        concat_axis=0,
        tiled=True,
    )
    slot_count = arrived.shape[1]
    grouped = arrived.reshape(seq_count * head_devs, exp_dev, slot_count, model_width)
    answered = run_experts(grouped, w_gate, w_up, w_down)
    returned = lax.all_to_all(
        answered.reshape(arrived.shape), ("seq", "head"), split_axis=0, concat_axis=0, tiled=True
    )
    outputs = returned.reshape(expert_count * capacity, model_width)[targets].reshape(
        row_count, top_count, model_width
    )
    expert_sum = jnp.sum(gate_weights[:, :, None] * outputs.astype(jnp.float32), axis=1).astype(
        jnp.bfloat16
    )
    return (hidden, expert_sum)


def solution(mesh):
    placed = (
        P(("groups", "seq"), "head"),
        P(("groups", "seq"), "head"),
        P(("groups", "seq"), "head"),
        P(("groups", "seq")),
        P("head", None, None),
        P("head"),
        P(("groups", "seq", "head"), None),
        P("head", None),
        P(),
        P(),
        P(("seq", "head"), None, None),
        P(("seq", "head"), None, None),
        P(("seq", "head"), None, None),
        P(("groups", "seq", "head"), None),
    )
    return jax.shard_map(
        shards,
        mesh=mesh,
        in_specs=placed,
        out_specs=(P(("groups", "seq", "head"), None), P(("groups", "seq", "head"), None)),
        check_vma=False,
    )
```

profile of v0, /device:TPU:13, one launch (start us, length us, event | category | flops | bytes accessed | tf_op | source)
XLA Modules:
  0.0 469.5 jit_solution(16345047846315380968)
XLA Ops:
  7.2 1.3 dynamic-slice
  8.6 1.9 fusion.55
  10.5 1.3 compare_convert_fusion.1
  11.8 2.2 fusion.24
  14.0 1.5 fusion.32
  15.5 0.7 all-gather.4.cloned.1.call-update
  16.2 7.9 %all-reduce = s32[8]{0:T(128)S(1)} all-reduce(s32[8]{0:T(128)S(1)} %get-tuple-element.53), channel_id=1, replica_groups=mesh['groups'=2,'seq'=8,'head'=2] {'seq'}, use_global_device_ids=true, to_apply=%add | all-reduce | flops 8 | bytes 64
  24.4 4.5 reduce-window.6
  29.5 1.6 fusion.5
  31.3 2.1 fusion.21
  33.4 104.6 %all-gather.6.cloned.1.call-done = f32[64,256,128]{2,1,0:T(8,128)} async-done(((f32[8,256,128]{2,1,0:T(8,128)}), f32[64,256,128]{2,1,0:T(8,128)}) %all-gather.6.cloned.1.call-update) | async-done | bytes 8388624 | tf_op jit(solution)/shard_map/all_gather | solution.py:9
  138.0 10.8 %while.12 = (s32[]{:T(128)}, s32[]{:T(128)}, f32[8,256,128]{2,1,0:T(8,128)S(1)}, s32[]{:T(128)}, s32[8]{0:T(128)S(1)}, /*index=5*/f32[8,8,256,128]{3,2,1,0:T(8,128)}, s32[]{:T(128)}, s32[]{:T(128)}, s32[]{:T(128)}) while((s32[]{:T(128)}, s32[]{:T(128)}, f32[8,256,128]{2,1,0:T(8,128)S(1)}, s32[]{:T(128)}, s32[8]{0:T(128)S(1)}, ...), condition=%wide.region_1.2_spmd, body=%wide.region_0.1_spmd.sunk | while | flops 524295 | bytes 3145905 | solution.py:17
  139.3 1.6 bitcast_add_fusion.2
  141.6 0.6 dynamic_slice.12
  142.9 1.6 bitcast_add_fusion.2
  146.4 1.7 bitcast_add_fusion.2
  148.8 3.5 fusion.28
  152.3 2.8 multiply_reduce_fusion
  155.5 0.9 copy.73
  156.4 4.6 all-to-all-start
  160.9 0.6 all-gather.4.cloned.1.call-done
  161.6 0.7 all-to-all-done
  162.3 4.8 %fusion.29 = (f32[128]{0:T(128)S(1)}, bf16[128,2048]{1,0:T(8,128)(2,1)S(1)}) fusion(bf16[128,2048]{0,1:T(8,128)(2,1)S(1)} %bitcast.136, bf16[2048,2048]{1,0:T(8,128)(2,1)} %all-gather.4.cloned.1.call-done, bf16[128,2048]{1,0:T(8,128)(2,1)S(1)} %copy-done.3), kind=kOutput, calls=%fused_computation.42 | convolution fusion | flops 1075314560 | bytes 9961984 | tf_op jit(solution)/shard_map/dot_general | solution.py:95
  167.1 1.6 convolution_convert_fusion
  168.8 134.7 %all_to_all.26 = bf16[16,80,2048]{2,1,0:T(8,128)(2,1)S(1)} all-to-all(bf16[16,80,2048]{2,1,0:T(8,128)(2,1)S(1)} %bitcast.135), channel_id=1, replica_groups=mesh['groups'=2,'seq'=8,'head'=2] {'seq','head'}, dimensions={0} | all-to-all | bytes 10485760 | tf_op jit(solution)/shard_map/all_to_all | solution.py:130
  303.5 5.6 %fusion.8 = f32[16,80,1024]{2,1,0:T(8,128)S(1)} fusion(bf16[16,80,2048]{2,1,0:T(8,128)(2,1)S(1)} %all_to_all.26, bf16[1,2048,1024]{2,1,0:T(8,128)(2,1)S(1)} %copy-done.10), kind=kOutput, calls=%fused_computation.20 | convolution fusion | flops 5368709120 | bytes 14680064 | tf_op jit(solution)/shard_map/gecd,edf->gecf/dot_general | solution.py:33
  309.1 6.4 %fusion.1 = bf16[16,1,80,1024]{3,2,0,1:T(8,128)(2,1)S(1)} fusion(f32[16,80,1024]{2,1,0:T(8,128)S(1)} %fusion.8, bf16[16,80,2048]{2,1,0:T(8,128)(2,1)S(1)} %all_to_all.26, bf16[1,2048,1024]{2,1,0:T(8,128)(2,1)S(1)} %copy-done.11), kind=kOutput, calls=%fused_computation.10 | convolution fusion | flops 5376573440 | bytes 17301504 | tf_op jit(solution)/shard_map/gecd,edf->gecf/dot_general | solution.py:32
  315.5 7.3 %fusion.12 = bf16[16,80,2048]{2,1,0:T(8,128)(2,1)} fusion(bf16[1,1024,2048]{2,1,0:T(8,128)(2,1)S(1)} %copy-done.12, bf16[16,1,80,1024]{3,2,0,1:T(8,128)(2,1)S(1)} %fusion.1), kind=kOutput, calls=%fused_computation.24 | convolution fusion | flops 5371330560 | bytes 12058624 | tf_op jit(solution)/shard_map/gecf,efd->gecd/dot_general | solution.py:35
  322.8 5.4 %all-to-all-start.2 = ((bf16[16,80,2048]{2,1,0:T(8,128)(2,1)}), bf16[16,80,2048]{2,1,0:T(8,128)(2,1)}, u32[]{:S(2)}, u32[]{:S(2)}) async-start(bf16[16,80,2048]{2,1,0:T(8,128)(2,1)} %fusion.12), calls=%async_computation.2 | async-start | bytes 10485760 | tf_op jit(solution)/shard_map/all_to_all | solution.py:140
  328.9 114.3 %all-to-all-done.2 = bf16[16,80,2048]{2,1,0:T(8,128)(2,1)} async-done(((bf16[16,80,2048]{2,1,0:T(8,128)(2,1)}), bf16[16,80,2048]{2,1,0:T(8,128)(2,1)}, u32[]{:S(2)}, u32[]{:S(2)}) %all-to-all-start.2) | async-done | bytes 5242912 | tf_op jit(solution)/shard_map/all_to_all | solution.py:140
  443.2 12.1 %gather_fusion = bf16[1024,2048]{1,0:T(8,128)(2,1)} fusion(bf16[1280,2048]{1,0:T(8,128)(2,1)} %bitcast.30, s32[1024]{0:T(1024)S(1)} %broadcast_clamp_fusion), kind=kCustom, calls=%fused_computation | custom fusion | bytes 8392704 | tf_op jit(solution)/shard_map/gather | solution.py:143
  455.3 7.3 %fusion = bf16[128,2048]{1,0:T(8,128)(2,1)} fusion(bf16[1024,2048]{1,0:T(8,128)(2,1)} %gather_fusion, f32[128,8]{1,0:T(8,128)S(1)} %copy.74), kind=kLoop, calls=%fused_computation.3 | loop fusion | flops 6029312 | bytes 4722688 | tf_op jit(solution)/shard_map/reduce_sum | solution.py:146
  (64 shorter events, 3.3 us)
Async XLA Ops:
  7.2 4.6 copy-start
  7.2 6.8 %copy-start.4 = (bf16[256,1024]{1,0:T(8,128)(2,1)S(1)}, bf16[256,1024]{1,0:T(8,128)(2,1)}, u32[]{:S(2)}) copy-start(bf16[256,1024]{1,0:T(8,128)(2,1)} %param.18) | copy-start | bytes 1572868
  7.2 130.8 %all-gather.6.cloned.1.call-start = ((), (), s32[]{:S(2)}) async-start(), calls=%async_computation.4 | async-start | bytes 9437184 | tf_op jit(solution)/shard_map/all_gather | solution.py:9
  14.0 10.2 %copy-start.7 = (s32[128,8]{0,1:T(8,128)S(1)}, s32[128,8]{0,1:T(8,128)}, u32[]{:S(2)}) copy-start(s32[128,8]{0,1:T(8,128)} %param.29) | copy-start | bytes 12292
  14.0 17.2 %copy-start.6 = (s32[256]{0:T(256)S(1)}, s32[256]{0:T(256)}, u32[]{:S(2)}) copy-start(s32[256]{0:T(256)} %param.19) | copy-start | bytes 3076
  14.0 17.3 %copy-start.13 = (bf16[256,1024]{1,0:T(8,128)(2,1)S(1)}, bf16[256,1024]{1,0:T(8,128)(2,1)}, u32[]{:S(2)}) copy-start(bf16[256,1024]{1,0:T(8,128)(2,1)} %param.16) | copy-start | bytes 1572868
  15.5 146.1 %all-gather.4.cloned.1.call-start = ((), (), s32[]{:S(2)}) async-start(), calls=%async_computation.3 | async-start | bytes 12582912 | tf_op jit(solution)/shard_map/all_gather | solution.py:97
  138.0 14.3 %copy-start.5 = (bf16[256,1024]{1,0:T(8,128)(2,1)S(1)}, bf16[256,1024]{1,0:T(8,128)(2,1)}, u32[]{:S(2)}) copy-start(bf16[256,1024]{1,0:T(8,128)(2,1)} %param.18) | copy-start | bytes 1572868
  148.8 6.4 %copy-start.9 = (f32[1024]{0:T(1024)S(1)}, f32[1024]{0:T(1024)}, u32[]{:S(2)}) copy-start(f32[1024]{0:T(1024)} %param.21) | copy-start | bytes 12292
  152.3 10.0 %copy-start.3 = (bf16[128,2048]{1,0:T(8,128)(2,1)S(1)}, bf16[128,2048]{1,0:T(8,128)(2,1)}, u32[]{:S(2)}) copy-start(bf16[128,2048]{1,0:T(8,128)(2,1)} %param.22) | copy-start | bytes 1572868
  156.4 5.9 %all-to-all-start = ((bf16[2,128,1024]{1,2,0:T(8,128)(2,1)}), bf16[2,128,1024]{1,2,0:T(8,128)(2,1)S(1)}, u32[]{:S(2)}, u32[]{:S(2)}) async-start(bf16[2,128,1024]{1,2,0:T(8,128)(2,1)} %copy.73), calls=%async_computation | async-start | bytes 1048576 | tf_op jit(solution)/shard_map/all_to_all | solution.py:94
  162.3 4.8 %copy-start.8 = (f32[2048]{0:T(1024)S(1)}, f32[2048]{0:T(1024)}, u32[]{:S(2)}) copy-start(f32[2048]{0:T(1024)} %param.24) | copy-start | bytes 24580
  167.1 161.3 %copy-start.2 = (bf16[128,2048]{1,0:T(8,128)(2,1)}, bf16[128,2048]{1,0:T(8,128)(2,1)S(1)}, u32[]{:S(2)}) copy-start(bf16[128,2048]{1,0:T(8,128)(2,1)S(1)} %get-tuple-element.57) | copy-start | bytes 1572868
  168.8 134.7 %copy-start.10 = (bf16[1,2048,1024]{2,1,0:T(8,128)(2,1)S(1)}, bf16[1,2048,1024]{2,1,0:T(8,128)(2,1)}, u32[]{:S(2)}) copy-start(bf16[1,2048,1024]{2,1,0:T(8,128)(2,1)} %param.27) | copy-start | bytes 12582916
  303.5 5.6 %copy-start.11 = (bf16[1,2048,1024]{2,1,0:T(8,128)(2,1)S(1)}, bf16[1,2048,1024]{2,1,0:T(8,128)(2,1)}, u32[]{:S(2)}) copy-start(bf16[1,2048,1024]{2,1,0:T(8,128)(2,1)} %param.26) | copy-start | bytes 12582916
  309.1 6.4 %copy-start.12 = (bf16[1,1024,2048]{2,1,0:T(8,128)(2,1)S(1)}, bf16[1,1024,2048]{2,1,0:T(8,128)(2,1)}, u32[]{:S(2)}) copy-start(bf16[1,1024,2048]{2,1,0:T(8,128)(2,1)} %param.28) | copy-start | bytes 12582916
  322.8 5.6 %copy-start.14 = (bf16[2048,16]{0,1:T(8,128)(2,1)S(1)}, bf16[2048,16]{0,1:T(8,128)(2,1)}, u32[]{:S(2)}) copy-start(bf16[2048,16]{0,1:T(8,128)(2,1)} %param.25) | copy-start | bytes 196612
  322.8 120.4 %all-to-all-start.2 = ((bf16[16,80,2048]{2,1,0:T(8,128)(2,1)}), bf16[16,80,2048]{2,1,0:T(8,128)(2,1)}, u32[]{:S(2)}, u32[]{:S(2)}) async-start(bf16[16,80,2048]{2,1,0:T(8,128)(2,1)} %fusion.12), calls=%async_computation.2 | async-start | bytes 10485760 | tf_op jit(solution)/shard_map/all_to_all | solution.py:140
  443.2 19.4 %copy-start.1 = (bf16[8,128,256]{2,1,0:T(8,128)(2,1)S(1)}, bf16[8,128,256]{2,1,0:T(8,128)(2,1)}, u32[]{:S(2)}) copy-start(bf16[8,128,256]{2,1,0:T(8,128)(2,1)} %param.20) | copy-start | bytes 1572868
Sparse Core Ops, SparseCore 0:
  15.6 122.2 all-gather.5
  139.5 22.0 all-gather.3
where the time goes:
time: 470 us; the launch traced here: 469 us
  waiting for transfers between devices  221 us (47%)
  blocking collectives  143 us (30%)
  matrix products  38 us (8%)
  other arithmetic  20.4 us (4%)
  local copies, waits for them, and re-layouts  19.1 us (4%)
  between operations  14.4 us (3%)
  starting transfers between devices  10.1 us (2%)
    all_to_all x1, blocking collectives, shards(): lax.all_to_all(send_rows.reshape(expert_count, capacity, model_width), ('...  135 us
    all_to_all x1, waiting for transfers between devices, shards(): lax.all_to_all(answered.reshape(arrived.shape), ('seq', 'head'), split_ax...  114 us
    all_gather x1, waiting for transfers between devices, carried_in(): gathered = jax.tree.map(lambda a: lax.all_gather(a, axis), part)  105 us
    gather x1, local copies, waits for them, and re-layouts, shards(): returned.reshape(expert_count * capacity, model_width)[targets]  12.1 us
  transfers between devices with their start and end apart: 4, of which 4 were waited for; matrix products, arithmetic and copies ran while one was open for 5% of the time, Pallas kernels for 0%

commit v1 on v0

v1 whole, which is shorter than its diff:
```python
import jax
import jax.numpy as jnp
from jax import lax
from jax.sharding import PartitionSpec as P


def carried_in(last_seg, local_state, token_count):
    place = lax.axis_index("seq")
    blocks = lax.axis_size("seq")
    longest = token_count * blocks // 3
    reach = min(blocks - 1, max(1, (longest - 2) // token_count + 1))
    last_all = lax.all_gather(last_seg, "seq")

    def last_of(back):
        index = place - back
        return jnp.where(index >= 0, last_all[jnp.maximum(index, 0)], -1 - back)

    before = last_of(1)
    carried = None
    window = local_state
    span = 1
    covered = 0
    while covered < reach:
        shifted = lax.ppermute(
            window.astype(jnp.bfloat16), "seq", [(i, i + span) for i in range(blocks - span)]
        ).astype(jnp.float32)
        if carried is None:
            carried = shifted
        else:
            carried = carried + jnp.where(last_of(span) == before, shifted, 0.0)
        covered += span
        if covered < reach:
            window = window + jnp.where(last_of(span) == last_seg, shifted, 0.0)
        span *= 2
    return before, carried


def features_of(inputs, feature_map, head_count, head_dim):
    grouped = inputs.reshape(inputs.shape[0], head_count, head_dim)
    projected = jnp.einsum("thd,hdf->thf", grouped, feature_map, preferred_element_type=jnp.float32)
    return (jax.nn.elu(projected) + 1.0).astype(jnp.bfloat16)


def run_expert(rows, gate, w_gate, w_up, w_down):
    gate_pre = jnp.dot(rows, w_gate, preferred_element_type=jnp.float32)
    up_pre = jnp.dot(rows, w_up, preferred_element_type=jnp.float32)
    activated = (jax.nn.silu(gate_pre) * up_pre).astype(jnp.bfloat16)
    answer = jnp.dot(activated, w_down, preferred_element_type=jnp.float32)
    return answer * gate[:, None]


def shards(
    query_proj,
    key_proj,
    value_proj,
    segment_ids,
    feature_map,
    head_gain,
    residual,
    out_weight,
    norm_gain,
    router,
    w_gate,
    w_up,
    w_down,
    expert_ids,
):
    token_count = query_proj.shape[0]
    head_count = feature_map.shape[0]
    head_dim = feature_map.shape[1]
    query_feat = features_of(query_proj, feature_map, head_count, head_dim)
    key_feat = features_of(key_proj, feature_map, head_count, head_dim)
    values = value_proj.reshape(token_count, head_count, head_dim)
    last_seg = segment_ids[token_count - 1]
    tail_mask = (segment_ids == last_seg).astype(jnp.bfloat16)
    local_state = jnp.einsum(
        "thf,thd->hfd",
        key_feat * tail_mask[:, None, None],
        values,
        preferred_element_type=jnp.float32,
    )
    seg_before, state_before = carried_in(last_seg, local_state, token_count)
    scores = jnp.einsum("thf,shf->hts", query_feat, key_feat, preferred_element_type=jnp.float32)
    positions = lax.iota(jnp.int32, token_count)
    allowed = (positions[None, :] <= positions[:, None]) & (
        segment_ids[None, :] == segment_ids[:, None]
    )
    block_weights = jnp.where(allowed[None], scores, 0.0).astype(jnp.bfloat16)
    within = jnp.einsum("hts,shd->thd", block_weights, values, preferred_element_type=jnp.float32)
    carried = jnp.einsum(
        "thf,hfd->thd",
        query_feat,
        state_before.astype(jnp.bfloat16),
        preferred_element_type=jnp.float32,
    )
    carry_mask = (segment_ids == seg_before).astype(jnp.float32)
    mixed = within + carry_mask[:, None, None] * carried
    scale = lax.rsqrt(jnp.mean(mixed * mixed, axis=2, keepdims=True) + 1e-06)
    attn_heads = (
        (mixed * scale * head_gain.reshape(head_count, head_dim))
        .reshape(token_count, head_count * head_dim)
        .astype(jnp.bfloat16)
    )
    attn_rows = lax.all_to_all(attn_heads, "head", split_axis=0, concat_axis=1, tiled=True)
    projected = jnp.dot(
        attn_rows,
        lax.all_gather(out_weight, "head", axis=0, tiled=True),
        preferred_element_type=jnp.float32,
    )
    hidden = (residual.astype(jnp.float32) + projected).astype(jnp.bfloat16)
    hidden_f = hidden.astype(jnp.float32)
    normed = (
        hidden_f
        * lax.rsqrt(jnp.mean(hidden_f * hidden_f, axis=1, keepdims=True) + 1e-05)
        * norm_gain
    ).astype(jnp.bfloat16)
    logits = jnp.dot(normed, router, preferred_element_type=jnp.float32)
    expert_count = router.shape[1]
    expert_iota = lax.iota(jnp.int32, expert_count)
    picked = expert_ids[:, :, None] == expert_iota[None, None, :]
    chosen = jnp.sum(jnp.where(picked, logits[:, None, :], 0.0), axis=2)
    gates = jax.nn.sigmoid(chosen)
    gate_weights = gates / jnp.sum(gates, axis=1, keepdims=True)
    dense_gates = jnp.sum(jnp.where(picked, gate_weights[:, :, None], 0.0), axis=1)
    spread = ("seq", "head")
    all_rows = lax.all_gather(normed, spread, axis=0, tiled=True)
    all_gates = lax.all_gather(dense_gates, spread, axis=0, tiled=True)
    exp_dev = w_gate.shape[0]
    first = (lax.axis_index("seq") * lax.axis_size("head") + lax.axis_index("head")) * exp_dev
    partial = 0.0
    for own in range(exp_dev):
        gate = jnp.sum(jnp.where(expert_iota[None, :] == first + own, all_gates, 0.0), axis=1)
        partial = partial + run_expert(all_rows, gate, w_gate[own], w_up[own], w_down[own])
    expert_sum = lax.psum_scatter(
        partial.astype(jnp.bfloat16), spread, scatter_dimension=0, tiled=True
    )
    return (hidden, expert_sum)


def solution(mesh):
    placed = (
        P(("groups", "seq"), "head"),
        P(("groups", "seq"), "head"),
        P(("groups", "seq"), "head"),
        P(("groups", "seq")),
        P("head", None, None),
        P("head"),
        P(("groups", "seq", "head"), None),
        P("head", None),
        P(),
        P(),
        P(("seq", "head"), None, None),
        P(("seq", "head"), None, None),
        P(("seq", "head"), None, None),
        P(("groups", "seq", "head"), None),
    )
    return jax.shard_map(
        shards,
        mesh=mesh,
        in_specs=placed,
        out_specs=(P(("groups", "seq", "head"), None), P(("groups", "seq", "head"), None)),
        check_vma=False,
    )
```

time: 470 us -> 290 us (0.62)
  the two profiles are of different devices: /device:TPU:13 before, /device:TPU:0 now
where the time goes in v1:
time: 290 us
  waiting for transfers between devices  168 us (58%)
  matrix products  54.9 us (19%)
  blocking collectives  37.9 us (13%)
  between operations  16 us (6%)
  starting transfers between devices  7.95 us (3%)
  other arithmetic  3.09 us (1%)
    reduce_scatter x1, waiting for transfers between devices, shards(): lax.psum_scatter(partial.astype(jnp.bfloat16), spread, scatter_dimension=...  102 us
    all_gather x1, waiting for transfers between devices, shards(): all_rows = lax.all_gather(normed, spread, axis=0, tiled=True)  51.7 us
    dot_general x1, matrix products, run_expert(): answer = jnp.dot(activated, w_down, preferred_element_type=jnp.float32)  26 us
    all_gather x1, blocking collectives, shards(): all_gates = lax.all_gather(dense_gates, spread, axis=0, tiled=True)  20.6 us
    dot_general x1, matrix products, run_expert(): gate_pre = jnp.dot(rows, w_gate, preferred_element_type=jnp.float32)  14.4 us
    unnamed x1, blocking collectives  13.1 us
    ppermute x2, waiting for transfers between devices, carried_in(): lax.ppermute(window.astype(jnp.bfloat16), 'seq', [(i, i + span) for i in...  12.9 us
    ppermute x2, starting transfers between devices, carried_in(): lax.ppermute(window.astype(jnp.bfloat16), 'seq', [(i, i + span) for i in...  7.83 us
  transfers between devices with their start and end apart: 5, of which 4 were waited for; matrix products, arithmetic and copies ran while one was open for 5% of the time, Pallas kernels for 0%

profile of v1, /device:TPU:0, one launch (start us, length us, event | category | flops | bytes accessed | tf_op | source)
XLA Modules:
  0.0 290.1 jit_solution(12551976899202699490)
XLA Ops:
  7.3 0.7 all-gather.3.cloned.1.call-update
  8.0 0.0 all-gather.5.cloned.1.call-start
  8.0 0.6 dynamic-slice
  8.6 1.2 slice_dynamic-update-slice_fusion
  9.9 13.1 %all-reduce = s32[8]{0:T(128)S(1)} all-reduce(s32[8]{0:T(128)S(1)} %get-tuple-element.4), channel_id=1, replica_groups=mesh['groups'=2,'seq'=8,'head'=2] {'seq'}, use_global_device_ids=true, to_apply=%add | all-reduce | flops 8 | bytes 64
  22.9 0.6 fusion.43
  24.2 0.7 compare_convert_fusion.1
  24.9 1.1 fusion.12
  26.1 1.2 fusion.44
  27.3 3.4 %collective-permute-start = (bf16[8,256,128]{2,1,0:T(8,128)(2,1)}, bf16[8,256,128]{2,1,0:T(8,128)(2,1)S(1)}, u32[]{:S(2)}, u32[]{:S(2)}) collective-permute-start(bf16[8,256,128]{2,1,0:T(8,128)(2,1)} %get-tuple-element.8), channel_id=1, source_target_pairs={{0,2},{2,4},{4,6},{6,8},{8,10},{10,12},{12,14},{1,3},{3,5},{5,7},{... | collective-permute-start | bytes 1572872 | tf_op jit(solution)/shard_map/ppermute | solution.py:24
  31.4 7.9 %collective-permute-done = bf16[8,256,128]{2,1,0:T(8,128)(2,1)S(1)} collective-permute-done((bf16[8,256,128]{2,1,0:T(8,128)(2,1)}, bf16[8,256,128]{2,1,0:T(8,128)(2,1)S(1)}, u32[]{:S(2)}, u32[]{:S(2)}) %collective-permute-start) | collective-permute-done | bytes 524320 | tf_op jit(solution)/shard_map/ppermute | solution.py:24
  39.3 0.9 fusion.18
  40.2 4.4 %collective-permute-start.1 = (bf16[8,256,128]{2,1,0:T(8,128)(2,1)}, bf16[8,256,128]{2,1,0:T(8,128)(2,1)S(1)}, u32[]{:S(2)}, u32[]{:S(2)}) collective-permute-start(bf16[8,256,128]{2,1,0:T(8,128)(2,1)} %fusion.18), channel_id=1, source_target_pairs={{0,4},{2,6},{4,8},{6,10},{8,12},{10,14},{1,5},{3,7},{5,9},{7,11},{... | collective-permute-start | bytes 1572872 | tf_op jit(solution)/shard_map/ppermute | solution.py:24
  45.3 0.1 fusion.39
  45.4 2.2 fusion.9
  47.6 5.0 %collective-permute-done.1 = bf16[8,256,128]{2,1,0:T(8,128)(2,1)S(1)} collective-permute-done((bf16[8,256,128]{2,1,0:T(8,128)(2,1)}, bf16[8,256,128]{2,1,0:T(8,128)(2,1)S(1)}, u32[]{:S(2)}, u32[]{:S(2)}) %collective-permute-start.1) | collective-permute-done | bytes 524320 | tf_op jit(solution)/shard_map/ppermute | solution.py:24
  52.6 1.4 fusion.16
  54.0 2.5 multiply_reduce_fusion
  56.6 0.2 multiply_convert_fusion.2
  56.8 0.1 convert_element_type.67
  56.9 0.1 copy.47
  57.0 4.2 %all_to_all.16 = bf16[2,128,1024]{1,2,0:T(8,128)(2,1)S(1)} all-to-all(bf16[2,128,1024]{1,2,0:T(8,128)(2,1)S(1)} %copy.47), channel_id=1, replica_groups=mesh['groups'=2,'seq'=8,'head'=2] {'head'}, dimensions={0} | all-to-all | bytes 1048576 | tf_op jit(solution)/shard_map/all_to_all | solution.py:104
  61.2 4.8 %fusion.20 = (f32[128]{0:T(128)S(1)}, bf16[128,2048]{1,0:T(8,128)(2,1)S(1)}) fusion(bf16[128,2048]{0,1:T(8,128)(2,1)S(1)} %bitcast.71, bf16[2048,2048]{1,0:T(8,128)(2,1)} %all-gather.3.cloned.1.call-done, bf16[128,2048]{1,0:T(8,128)(2,1)S(1)} %copy-done.3), kind=kOutput, calls=%fused_computation.32 | convolution fusion | flops 1075314560 | bytes 9961984 | tf_op jit(solution)/shard_map/dot_general | solution.py:105
  66.0 1.0 fusion.22
  67.0 0.0 reduce-scatter.2.cloned.1.call-start
  67.1 1.3 fusion.45
  68.5 20.6 %all_gather.15 = f32[2048,16]{0,1:T(8,128)S(1)} all-gather(f32[128,16]{0,1:T(8,128)S(1)} %select_reduce_fusion.1), channel_id=1, replica_groups=mesh['groups'=2,'seq'=8,'head'=2] {'seq','head'}, dimensions={0}, use_global_device_ids=true | all-gather | bytes 139264 | tf_op jit(solution)/shard_map/all_gather | solution.py:127
  89.1 0.1 select_reduce_fusion
  89.2 51.7 %all-gather.5.cloned.1.call-done = bf16[2048,2048]{1,0:T(8,128)(2,1)} async-done(((bf16[128,2048]{1,0:T(8,128)(2,1)}), bf16[2048,2048]{1,0:T(8,128)(2,1)}) %all-gather.5.cloned.1.call-update) | async-done | bytes 8388624 | tf_op jit(solution)/shard_map/all_gather | solution.py:126
  140.9 14.4 %fusion.3 = f32[2048,1024]{1,0:T(8,128)} fusion(bf16[2048,2048]{1,0:T(8,128)(2,1)} %all-gather.5.cloned.1.call-done, bf16[1,2048,1024]{2,1,0:T(8,128)(2,1)} %param.24), kind=kOutput, calls=%fused_computation.8 | convolution fusion | flops 8589934592 | bytes 20971520 | tf_op jit(solution)/shard_map/dot_general | solution.py:45
  155.3 26.0 %multiply_convert_fusion = bf16[2048,2048]{1,0:T(8,128)(2,1)} fusion(f32[2048]{0:T(1024)S(1)} %select_reduce_fusion, f32[2048,1024]{1,0:T(8,128)} %fusion.3, bf16[2048,2048]{1,0:T(8,128)(2,1)} %all-gather.5.cloned.1.call-done, bf16[1,1024,2048]{2,1,0:T(8,128)(2,1)} %param.26, bf16[1,2048,1024]{2,1,0:T(8,128)(2,1)} %param.25), kind=kOutput, calls=%fused_computation | convolution fusion | flops 17200840704 | bytes 33562624 | tf_op jit(solution)/shard_map/dot_general | solution.py:48
  181.3 102.2 %reduce-scatter.2.cloned.1.call-done = bf16[128,2048]{1,0:T(8,128)(2,1)} async-done(((bf16[2048,2048]{1,0:T(8,128)(2,1)}), bf16[128,2048]{1,0:T(8,128)(2,1)}) %reduce-scatter.2.cloned.1.call-update) | async-done | bytes 524304 | tf_op jit(solution)/shard_map/reduce_scatter | solution.py:134
  (36 shorter events, 0.3 us)
Async XLA Ops:
  7.2 17.7 %copy-start = (bf16[8,128,256]{2,1,0:T(8,128)(2,1)S(1)}, bf16[8,128,256]{2,1,0:T(8,128)(2,1)}, u32[]{:S(2)}) copy-start(bf16[8,128,256]{2,1,0:T(8,128)(2,1)} %param.18) | copy-start | bytes 1572868
  7.2 0.8 copy-start.11
  7.2 1.4 copy-start.7
  7.2 17.7 %copy-start.10 = (bf16[256,1024]{1,0:T(8,128)(2,1)S(1)}, bf16[256,1024]{1,0:T(8,128)(2,1)}, u32[]{:S(2)}) copy-start(bf16[256,1024]{1,0:T(8,128)(2,1)} %param.15) | copy-start | bytes 1572868
  7.2 18.8 %copy-start.4 = (bf16[256,1024]{1,0:T(8,128)(2,1)S(1)}, bf16[256,1024]{1,0:T(8,128)(2,1)}, u32[]{:S(2)}) copy-start(bf16[256,1024]{1,0:T(8,128)(2,1)} %param.16) | copy-start | bytes 1572868
  7.2 53.9 %all-gather.3.cloned.1.call-start = ((), (), s32[]{:S(2)}) async-start(), calls=%async_computation.2 | async-start | bytes 12582912 | tf_op jit(solution)/shard_map/all_gather | solution.py:107
  8.0 133.0 %all-gather.5.cloned.1.call-start = ((), (), s32[]{:S(2)}) async-start(), calls=%async_computation.3 | async-start | bytes 8912896 | tf_op jit(solution)/shard_map/all_gather | solution.py:126
  27.3 12.0 %collective-permute-start = (bf16[8,256,128]{2,1,0:T(8,128)(2,1)}, bf16[8,256,128]{2,1,0:T(8,128)(2,1)S(1)}, u32[]{:S(2)}, u32[]{:S(2)}) collective-permute-start(bf16[8,256,128]{2,1,0:T(8,128)(2,1)} %get-tuple-element.8), channel_id=1, source_target_pairs={{0,2},{2,4},{4,6},{6,8},{8,10},{10,12},{12,14},{1,3},{3,5},{5,7},{... | collective-permute-start | bytes 1572872 | tf_op jit(solution)/shard_map/ppermute | solution.py:24
  40.2 12.3 %collective-permute-start.1 = (bf16[8,256,128]{2,1,0:T(8,128)(2,1)}, bf16[8,256,128]{2,1,0:T(8,128)(2,1)S(1)}, u32[]{:S(2)}, u32[]{:S(2)}) collective-permute-start(bf16[8,256,128]{2,1,0:T(8,128)(2,1)} %fusion.18), channel_id=1, source_target_pairs={{0,4},{2,6},{4,8},{6,10},{8,12},{10,14},{1,5},{3,7},{5,9},{7,11},{... | collective-permute-start | bytes 1572872 | tf_op jit(solution)/shard_map/ppermute | solution.py:24
  47.5 5.0 %copy-start.2 = (bf16[256,8,256]{0,2,1:T(8,128)(2,1)}, bf16[256,8,256]{0,2,1:T(8,128)(2,1)S(1)}, u32[]{:S(2)}) copy-start(bf16[256,8,256]{0,2,1:T(8,128)(2,1)S(1)} %fusion.9) | copy-start | bytes 3145732
  47.5 9.0 %copy-start.9 = (f32[1024]{0:T(1024)S(1)}, f32[1024]{0:T(1024)}, u32[]{:S(2)}) copy-start(f32[1024]{0:T(1024)} %param.19) | copy-start | bytes 12292
  54.0 7.1 %copy-start.3 = (bf16[128,2048]{1,0:T(8,128)(2,1)S(1)}, bf16[128,2048]{1,0:T(8,128)(2,1)}, u32[]{:S(2)}) copy-start(bf16[128,2048]{1,0:T(8,128)(2,1)} %param.20) | copy-start | bytes 1572868
  61.1 4.9 %copy-start.8 = (f32[2048]{0:T(1024)S(1)}, f32[2048]{0:T(1024)}, u32[]{:S(2)}) copy-start(f32[2048]{0:T(1024)} %param.22) | copy-start | bytes 24580
  61.1 5.9 %copy-start.5 = (bf16[2048,16]{0,1:T(8,128)(2,1)S(1)}, bf16[2048,16]{0,1:T(8,128)(2,1)}, u32[]{:S(2)}) copy-start(bf16[2048,16]{0,1:T(8,128)(2,1)} %param.23) | copy-start | bytes 196612
  61.1 7.2 %copy-start.6 = (s32[128,8]{0,1:T(8,128)S(1)}, s32[128,8]{0,1:T(8,128)}, u32[]{:S(2)}) copy-start(s32[128,8]{0,1:T(8,128)} %param.27) | copy-start | bytes 12292
  66.0 89.4 %copy-start.1 = (bf16[128,2048]{1,0:T(8,128)(2,1)}, bf16[128,2048]{1,0:T(8,128)(2,1)S(1)}, u32[]{:S(2)}) copy-start(bf16[128,2048]{1,0:T(8,128)(2,1)S(1)} %get-tuple-element.13) | copy-start | bytes 1572868
  67.0 216.5 %reduce-scatter.2.cloned.1.call-start = ((), (), s32[]{:S(2)}) async-start(), calls=%async_computation.4 | async-start | bytes 8912896 | tf_op jit(solution)/shard_map/reduce_scatter | solution.py:134
Sparse Core Ops, SparseCore 0:
  9.6 22.5 all-gather.2
  67.1 73.7 all-gather.4
  181.5 102.0 reduce-scatter.1

commit v2 on v1

--- a/solution.py
+++ b/solution.py
@@ -1,36 +1,41 @@
+import functools
+
 import jax
 import jax.numpy as jnp
 from jax import lax
+from jax.experimental import pallas as pl
+from jax.experimental.pallas import tpu as pltpu
 from jax.sharding import PartitionSpec as P
 
 
 def carried_in(last_seg, local_state, token_count):
-    place = lax.axis_index("seq")
     blocks = lax.axis_size("seq")
     longest = token_count * blocks // 3
     reach = min(blocks - 1, max(1, (longest - 2) // token_count + 1))
-    last_all = lax.all_gather(last_seg, "seq")
-
-    def last_of(back):
-        index = place - back
-        return jnp.where(index >= 0, last_all[jnp.maximum(index, 0)], -1 - back)
-
-    before = last_of(1)
+    state_rows = local_state.shape[0] * local_state.shape[1]
+    width = local_state.shape[2]
+    before = None
     carried = None
     window = local_state
     span = 1
     covered = 0
     while covered < reach:
-        shifted = lax.ppermute(
-            window.astype(jnp.bfloat16), "seq", [(i, i + span) for i in range(blocks - span)]
-        ).astype(jnp.float32)
+        packet = jnp.concatenate(
+            [
+                window.reshape(state_rows, width).astype(jnp.bfloat16),
+                jnp.full((16, width), last_seg, jnp.bfloat16),
+            ]
+        )
+        arrived = lax.ppermute(packet, "seq", [(i, i + span) for i in range(blocks - span)])
+        shifted = arrived[:state_rows].astype(jnp.float32).reshape(local_state.shape)
+        seg = arrived[state_rows, 0].astype(jnp.int32)
         if carried is None:
-            carried = shifted
+            before, carried = seg, shifted
         else:
-            carried = carried + jnp.where(last_of(span) == before, shifted, 0.0)
+            carried = carried + jnp.where(seg == before, shifted, 0.0)
         covered += span
         if covered < reach:
-            window = window + jnp.where(last_of(span) == last_seg, shifted, 0.0)
+            window = window + jnp.where(seg == last_seg, shifted, 0.0)
         span *= 2
     return before, carried
 
@@ -49,7 +54,324 @@
     return answer * gate[:, None]
 
 
+MESH = pl.DeviceIdType.MESH
+TILE = 256
+VMEM_MOST = 63 * 1024 * 1024
+
+
+def ring_place(index, count, folded):
+    if not folded:
+        return index
+    far, side = index // 2, index % 2
+    return far + side * (count - 1 - 2 * far)
+
+
+def ring_index(place, count, folded):
+    if not folded:
+        return place
+    side = place // (count // 2)
+    far = place + side * (count - 1 - 2 * place)
+    return 2 * far + side
+
+
+def moe_kernel(
+    count,
+    folded,
+    experts,
+    x_ref,
+    wg_hbm,
+    wu_hbm,
+    wd_hbm,
+    out_ref,
+    rows_buf,
+    part,
+    pair,
+    inbox,
+    wg,
+    wu,
+    wd,
+    act,
+    load_sem,
+    ag_send,
+    ag_recv,
+    sib_send,
+    sib_recv,
+    rs_send,
+    rs_recv,
+    pair_send,
+    pair_recv,
+):
+    rows, padded = x_ref.shape
+    width = out_ref.shape[1]
+    half = rows // 2
+    far = count // 2
+    core = lax.axis_index("head")
+    seq = lax.axis_index("seq")
+    place = ring_place(seq, count, folded)
+    ahead = {"seq": ring_index((place + 1) % count, count, folded)}
+    behind = {"seq": ring_index((place + count - 1) % count, count, folded)}
+    sibling = {"head": 1 - core}
+    toward = (ahead, behind)
+
+    loads = [
+        pltpu.make_async_copy(src.at[0], dst, load_sem.at[i])
+        for i, (src, dst) in enumerate(((wg_hbm, wg), (wu_hbm, wu), (wd_hbm, wd)))
+    ]
+    for load in loads:
+        load.start()
+
+    barrier = pltpu.get_barrier_semaphore()
+    for other in (ahead, behind, sibling):
+        pl.semaphore_signal(barrier, inc=1, device_id=other, device_id_type=MESH)
+    pl.semaphore_wait(barrier, 3)
+
+    def spot(slot):
+        if slot == 0:
+            return 0
+        if slot == far:
+            return count - 1
+        return 2 * slot - 1 if slot < far else 2 * (count - slot)
+
+    def start_row(slot, which, part_of=0):
+        return pl.multiple_of((spot(slot) * 2 + which) * rows + part_of * half, half)
+
+    def block(ref, slot, which):
+        return ref.at[pl.ds(start_row(slot, which), rows)]
+
+    def chunk(ref, slot, which, h):
+        return ref.at[pl.ds(start_row(slot, which, h), half)]
+
+    def slot_of(way, hop):
+        return hop if way == 0 else (count - hop) % count
+
+    own_copy = pltpu.make_async_copy(x_ref, block(rows_buf, 0, core), load_sem.at[3])
+    own_copy.start()
+
+    gathers = {}
+    for way in range(2):
+        for hop in range(far):
+            for h in range(2):
+                if hop == far - 1 and h != way:
+                    continue
+                if hop == 0:
+                    src = x_ref.at[pl.ds(h * half, half)]
+                else:
+                    src = chunk(rows_buf, slot_of(way, hop), core, h)
+                gathers[way, hop, h] = pltpu.make_async_remote_copy(
+                    src_ref=src,
+                    dst_ref=chunk(rows_buf, slot_of(way, hop + 1), core, h),
+                    send_sem=ag_send.at[way, hop, h],
+                    recv_sem=ag_recv.at[way, hop, h],
+                    device_id=toward[way],
+                    device_id_type=MESH,
+                )
+
+    shares = {}
+    answers = {}
+    for slot in range(count):
+        src = x_ref if slot == 0 else block(rows_buf, slot, core)
+        shares[slot] = pltpu.make_async_remote_copy(
+            src_ref=src,
+            dst_ref=block(rows_buf, slot, core),
+            send_sem=sib_send.at[slot],
+            recv_sem=sib_recv.at[slot],
+            device_id=sibling,
+            device_id_type=MESH,
+        )
+        answers[slot] = pltpu.make_async_remote_copy(
+            src_ref=block(part, slot, 1 - core),
+            dst_ref=pair.at[slot],
+            send_sem=pair_send.at[slot],
+            recv_sem=pair_recv.at[slot],
+            device_id=sibling,
+            device_id_type=MESH,
+        )
+
+    def compute(first_slot, blocks):
+        low = spot(first_slot) * 2 * rows
+        tall = blocks * 2 * rows
+        expert = lax.axis_index("seq") * 2 + core
+        taken = pl.ds(low, tall)
+        extra = rows_buf[taken, width:].astype(jnp.float32)
+        lane = lax.broadcasted_iota(jnp.int32, extra.shape, 1)
+        mine = (lane == expert) | (lane == expert + experts)
+        gate = jnp.sum(jnp.where(mine, extra, 0.0), axis=1, keepdims=True)
+
+        def up_step(t, carry):
+            cols = pl.ds(pl.multiple_of(t * TILE, TILE), TILE)
+            x = rows_buf[taken, :width]
+            gate_pre = jnp.dot(x, wg[:, cols], preferred_element_type=jnp.float32)
+            up_pre = jnp.dot(x, wu[:, cols], preferred_element_type=jnp.float32)
+            act[:tall, cols] = (gate_pre * jax.nn.sigmoid(gate_pre) * up_pre).astype(jnp.bfloat16)
+            return carry
+
+        lax.fori_loop(0, wg.shape[1] // TILE, up_step, 0)
+
+        def down_step(t, carry):
+            cols = pl.ds(pl.multiple_of(t * TILE, TILE), TILE)
+            answer = jnp.dot(act[:tall, :], wd[:, cols], preferred_element_type=jnp.float32)
+            part[taken, cols] = (answer * gate).astype(jnp.bfloat16)
+            return carry
+
+        lax.fori_loop(0, width // TILE, down_step, 0)
+
+    sums = {}
+    for way in range(2):
+        for hop in range(far, 0, -1):
+            for h in range(2):
+                if hop == far and h != way:
+                    continue
+                sums[way, hop, h] = pltpu.make_async_remote_copy(
+                    src_ref=chunk(part, slot_of(way, hop), core, h),
+                    dst_ref=inbox.at[way, hop - 1, h],
+                    send_sem=rs_send.at[way, hop - 1, h],
+                    recv_sem=rs_recv.at[way, hop - 1, h],
+                    device_id=toward[1 - way],
+                    device_id_type=MESH,
+                )
+
+    def add_and_send(way, hop, h):
+        slot = slot_of(way, hop)
+        here = pl.ds(start_row(slot, core, h), half)
+        total = part[here, :].astype(jnp.float32) + pair[slot, h * half : (h + 1) * half, :].astype(
+            jnp.float32
+        )
+        if (way, hop + 1, h) in sums:
+            sums[way, hop + 1, h].wait_recv()
+            total = total + inbox[way, hop, h].astype(jnp.float32)
+        part[here, :] = total.astype(jnp.bfloat16)
+        sums[way, hop, h].start()
+
+    for h in range(2):
+        for way in range(2):
+            at = h if way == 0 else 1 - h
+            if (way, 0, at) in gathers:
+                gathers[way, 0, at].start()
+    shares[0].start()
+    for load in loads:
+        load.wait()
+    own_copy.wait()
+    shares[0].wait_recv()
+    compute(0, 1)
+    answers[0].start()
+    for hop in range(1, far + 1):
+        for h in range(2):
+            for way in range(2):
+                at = h if way == 0 else 1 - h
+                if (way, hop - 1, at) in gathers:
+                    gathers[way, hop - 1, at].wait_recv()
+                if (way, hop, at) in gathers:
+                    gathers[way, hop, at].start()
+        slots = (hop, count - hop) if hop < far else (far,)
+        for slot in slots:
+            shares[slot].start()
+        for slot in slots:
+            shares[slot].wait_recv()
+        compute(hop, len(slots))
+        for slot in slots:
+            answers[slot].start()
+        if hop == far - 1:
+            for way in range(2):
+                answers[slot_of(way, hop)].wait_recv()
+            for way in range(2):
+                add_and_send(way, hop, 1 - way)
+
+    answers[far].wait_recv()
+    for way in range(2):
+        add_and_send(way, far, way)
+    for way in range(2):
+        add_and_send(way, far - 1, way)
+    for hop in range(far - 2, 0, -1):
+        for way in range(2):
+            answers[slot_of(way, hop)].wait_recv()
+        for turn in range(2):
+            for way in range(2):
+                add_and_send(way, hop, 1 - way if turn == 0 else way)
+    answers[0].wait_recv()
+    for h in range(2):
+        here = pl.ds(start_row(0, core, h), half)
+        total = part[here, :].astype(jnp.float32) + pair[0, h * half : (h + 1) * half, :].astype(
+            jnp.float32
+        )
+        for way in range(2):
+            if (way, 1, h) in sums:
+                sums[way, 1, h].wait_recv()
+                total = total + inbox[way, 0, h].astype(jnp.float32)
+        out_ref[h * half : (h + 1) * half, :] = total.astype(out_ref.dtype)
+    for group in (gathers, shares, answers, sums):
+        for copy in group.values():
+            copy.wait_send()
+
+
+def moe_scratch(count, rows, padded, width, hidden):
+    half = rows // 2
+    far = count // 2
+    tall = count * 2 * rows
+    bf16 = jnp.bfloat16
+    return [
+        ((tall, padded), bf16),
+        ((tall, width), bf16),
+        ((count, rows, width), bf16),
+        ((2, far, 2, half, width), bf16),
+        ((width, hidden), bf16),
+        ((width, hidden), bf16),
+        ((hidden, width), bf16),
+        ((4 * rows, hidden), bf16),
+    ]
+
+
+def moe(rows_in, width, experts, w_gate, w_up, w_down, folded):
+    count = lax.axis_size("seq")
+    rows, padded = rows_in.shape
+    far = count // 2
+    dma = pltpu.SemaphoreType.DMA
+    scratch = moe_scratch(count, rows, padded, width, w_gate.shape[2])
+    tall = count * 2 * rows
+    return pl.pallas_call(
+        functools.partial(moe_kernel, count, folded, experts),
+        out_shape=jax.ShapeDtypeStruct((rows, width), jnp.bfloat16),
+        in_specs=[pl.BlockSpec(memory_space=pltpu.VMEM)]
+        + [pl.BlockSpec(memory_space=pl.ANY)] * 3,
+        out_specs=pl.BlockSpec(memory_space=pltpu.VMEM),
+        scratch_shapes=[pltpu.VMEM(shape, dtype) for shape, dtype in scratch]
+        + [
+            dma((4,)),
+            dma((2, far, 2)),
+            dma((2, far, 2)),
+            dma((count,)),
+            dma((count,)),
+            dma((2, far, 2)),
+            dma((2, far, 2)),
+            dma((count,)),
+            dma((count,)),
+        ],
+        compiler_params=pltpu.CompilerParams(
+            collective_id=0, has_side_effects=True, vmem_limit_bytes=VMEM_MOST
+        ),
+        cost_estimate=pl.CostEstimate(
+            flops=6 * tall * width * w_gate.shape[2],
+            bytes_accessed=6 * width * w_gate.shape[2],
+            transcendentals=tall * w_gate.shape[2],
+        ),
+    )(rows_in, w_gate, w_up, w_down)
+
+
+def moe_fits(count, heads, rows, padded, width, w_gate):
+    if heads != 2 or count < 4 or count % 2 or w_gate.shape[0] != 1:
+        return False
+    if rows % 32 or width % TILE or w_gate.shape[2] % TILE:
+        return False
+    need = 0
+    for shape, _ in moe_scratch(count, rows, padded, width, w_gate.shape[2]):
+        size = 2
+        for extent in shape:
+            size *= extent
+        need += size
+    return need < VMEM_MOST * 7 // 8
+
+
 def shards(
+    folded,
     query_proj,
     key_proj,
     value_proj,
@@ -101,12 +423,18 @@
         .reshape(token_count, head_count * head_dim)
         .astype(jnp.bfloat16)
     )
-    attn_rows = lax.all_to_all(attn_heads, "head", split_axis=0, concat_axis=1, tiled=True)
-    projected = jnp.dot(
-        attn_rows,
-        lax.all_gather(out_weight, "head", axis=0, tiled=True),
-        preferred_element_type=jnp.float32,
-    )
+    row_count = residual.shape[0]
+    head_place = lax.axis_index("head")
+    head_devs = lax.axis_size("head")
+    sums = jnp.dot(attn_heads, out_weight, preferred_element_type=jnp.float32)
+    projected = lax.dynamic_slice_in_dim(sums, head_place * row_count, row_count)
+    for step in range(1, head_devs):
+        target = (head_place + step) % head_devs
+        projected = projected + lax.ppermute(
+            lax.dynamic_slice_in_dim(sums, target * row_count, row_count),
+            "head",
+            [(i, (i + step) % head_devs) for i in range(head_devs)],
+        )
     hidden = (residual.astype(jnp.float32) + projected).astype(jnp.bfloat16)
     hidden_f = hidden.astype(jnp.float32)
     normed = (
@@ -122,6 +450,15 @@
     gates = jax.nn.sigmoid(chosen)
     gate_weights = gates / jnp.sum(gates, axis=1, keepdims=True)
     dense_gates = jnp.sum(jnp.where(picked, gate_weights[:, :, None], 0.0), axis=1)
+    model_width = normed.shape[1]
+    coarse = lax.reduce_precision(dense_gates, 8, 7)
+    lanes = -(-2 * expert_count // 128) * 128
+    extra = jnp.concatenate([coarse, dense_gates - coarse], axis=1).astype(jnp.bfloat16)
+    extra = jnp.pad(extra, ((0, 0), (0, lanes - 2 * expert_count)))
+    if moe_fits(lax.axis_size("seq"), head_devs, row_count, model_width + lanes, model_width, w_gate):
+        rows_in = jnp.concatenate([normed, extra], axis=1)
+        expert_sum = moe(rows_in, model_width, expert_count, w_gate, w_up, w_down, folded)
+        return (hidden, expert_sum)
     spread = ("seq", "head")
     all_rows = lax.all_gather(normed, spread, axis=0, tiled=True)
     all_gates = lax.all_gather(dense_gates, spread, axis=0, tiled=True)
@@ -135,6 +472,14 @@
         partial.astype(jnp.bfloat16), spread, scatter_dimension=0, tiled=True
     )
     return (hidden, expert_sum)
+
+
+def folded_seq(mesh):
+    chips = [getattr(d, "coords", None) for d in mesh.devices[0, :3, 0]]
+    if None in chips or len(chips) < 3:
+        return True
+    moved = [sum(abs(i - j) for i, j in zip(a, b)) for a, b in zip(chips, chips[1:])]
+    return moved[0] == 1 and moved[1] == 2
 
 
 def solution(mesh):
@@ -155,7 +500,7 @@
         P(("groups", "seq", "head"), None),
     )
     return jax.shard_map(
-        shards,
+        functools.partial(shards, folded_seq(mesh)),
         mesh=mesh,
         in_specs=placed,
         out_specs=(P(("groups", "seq", "head"), None), P(("groups", "seq", "head"), None)),

time: 290 us -> 167 us (0.58)
  waiting for transfers between devices: 168 us -> 22.3 us
  Pallas kernels: 0 us -> 105 us
  matrix products: 54.9 us -> 11.9 us
  blocking collectives: 37.9 us -> 0 us
  between operations: 16 us -> 3.54 us
  local copies, waits for them, and re-layouts: 2.73 us -> 7.44 us
    pallas_call x0 -> x1, Pallas kernels: none -> 105 us  [moe(): pl.pallas_call(functools.partial(moe_kernel, count, folded, experts), out...]
    reduce_scatter x1 -> x0, waiting for transfers between devices: 102 us -> none  [shards(): lax.psum_scatter(partial.astype(jnp.bfloat16), spread, scatter_dimension=...]
    all_gather x2 -> x0, waiting for transfers between devices: 51.7 us -> none  [the longest x1 51.7 us: shards(): all_rows = lax.all_gather(normed, spread, axis=0, tiled=True)]
    dot_general x3 -> x1, matrix products: 45.2 us -> 3.46 us  [shards(): sums = jnp.dot(attn_heads, out_weight, preferred_element_type=jnp.float32)]
    all_gather x1 -> x0, blocking collectives: 20.6 us -> none  [shards(): all_gates = lax.all_gather(dense_gates, spread, axis=0, tiled=True)]
    unnamed x1 -> x0, blocking collectives: 13.1 us -> none
    ppermute x2 -> x3, waiting for transfers between devices: 12.9 us -> 22.3 us  [the longest x2 19.3 us: carried_in(): lax.ppermute(packet, 'seq', [(i, i + span) for i in range(blocks - span)])]
    all_to_all x1 -> x0, blocking collectives: 4.15 us -> none  [shards(): lax.all_to_all(attn_heads, 'head', split_axis=0, concat_axis=1, tiled=True)]
  transfers between devices with their start and end apart: 5 -> 3, of which waited for: 4 -> 3; matrix products, arithmetic and copies ran while one was open for 5% -> 1% of each run, Pallas kernels for 0% -> 0%
where the time goes in v2:
time: 167 us; the launch traced here: 166 us
  Pallas kernels  105 us (63%)
  waiting for transfers between devices  22.3 us (13%)
  matrix products  11.9 us (7%)
  starting transfers between devices  10.3 us (6%)
  local copies, waits for them, and re-layouts  7.44 us (4%)
  other arithmetic  5.91 us (4%)
  between operations  3.54 us (2%)
    pallas_call x1, Pallas kernels, moe(): pl.pallas_call(functools.partial(moe_kernel, count, folded, experts), out...  105 us
    ppermute x2, waiting for transfers between devices, carried_in(): lax.ppermute(packet, 'seq', [(i, i + span) for i in range(blocks - span)])  19.3 us
    ppermute x2, starting transfers between devices, carried_in(): lax.ppermute(packet, 'seq', [(i, i + span) for i in range(blocks - span)])  10.3 us
    dot_general x2, matrix products, features_of(): jnp.einsum('thd,hdf->thf', grouped, feature_map, preferred_element_type=j...  4.36 us
    unnamed x23, local copies, waits for them, and re-layouts  3.86 us
    dot_general x1, matrix products, shards(): sums = jnp.dot(attn_heads, out_weight, preferred_element_type=jnp.float32)  3.46 us
  transfers between devices with their start and end apart: 3, of which 3 were waited for; matrix products, arithmetic and copies ran while one was open for 1% of the time, Pallas kernels for 0%

profile of v2, /device:TPU:0, one launch (start us, length us, event | category | flops | bytes accessed | tf_op | source)
XLA Modules:
  0.0 166.3 jit_solution(8109668899538346141)
XLA Ops:
  0.6 0.0 copy-start
  0.6 1.3 slice.15
  2.0 1.3 compare_convert_fusion.1
  4.0 2.2 %fusion.5 = bf16[256,8,256]{0,2,1:T(8,128)(2,1)S(1)} fusion(bf16[8,128,256]{2,1,0:T(8,128)(2,1)S(1)} %copy-done, bf16[256,1024]{1,0:T(8,128)(2,1)} %param.15), kind=kOutput, calls=%fused_computation.9 | convolution fusion | flops 136839168 | bytes 2097152 | tf_op jit(solution)/shard_map/thd,hdf->thf/dot_general | solution.py:45
  6.2 0.4 fusion.32
  6.7 0.5 copy-done.2
  7.2 4.9 %collective-permute-start = (bf16[2064,128]{1,0:T(8,128)(2,1)S(1)}, bf16[2064,128]{1,0:T(8,128)(2,1)S(1)}, u32[]{:S(2)}, u32[]{:S(2)}) collective-permute-start(bf16[2064,128]{1,0:T(8,128)(2,1)S(1)} %concatenate.13), channel_id=1, source_target_pairs={{0,2},{2,4},{4,6},{6,8},{8,10},{10,12},{12,14},{1,3},{3,5},{5,7},{... | collective-permute-start | bytes 1585160 | tf_op jit(solution)/shard_map/ppermute | solution.py:29
  12.1 11.2 %collective-permute-done = bf16[2064,128]{1,0:T(8,128)(2,1)S(1)} collective-permute-done((bf16[2064,128]{1,0:T(8,128)(2,1)S(1)}, bf16[2064,128]{1,0:T(8,128)(2,1)S(1)}, u32[]{:S(2)}, u32[]{:S(2)}) %collective-permute-start) | collective-permute-done | bytes 528416 | tf_op jit(solution)/shard_map/ppermute | solution.py:29
  23.3 0.5 slice.20
  25.1 0.1 convert_select_fusion
  25.2 0.1 add_convert_fusion.1
  25.4 5.4 %collective-permute-start.1 = (bf16[2064,128]{1,0:T(8,128)(2,1)S(1)}, bf16[2064,128]{1,0:T(8,128)(2,1)S(1)}, u32[]{:S(2)}, u32[]{:S(2)}) collective-permute-start(bf16[2064,128]{1,0:T(8,128)(2,1)S(1)} %concatenate.14), channel_id=1, source_target_pairs={{0,4},{2,6},{4,8},{6,10},{8,12},{10,14},{1,5},{3,7},{5,9},{7,11},{... | collective-permute-start | bytes 1585160 | tf_op jit(solution)/shard_map/ppermute | solution.py:29
  30.8 0.1 fusion.29
  30.9 2.2 %fusion.2 = bf16[256,8,256]{0,2,1:T(8,128)(2,1)S(1)} fusion(bf16[8,128,256]{2,1,0:T(8,128)(2,1)S(1)} %copy-done, bf16[256,1024]{1,0:T(8,128)(2,1)} %param.14), kind=kOutput, calls=%fused_computation.6 | convolution fusion | flops 136839168 | bytes 2097152 | tf_op jit(solution)/shard_map/thd,hdf->thf/dot_general | solution.py:45
  33.1 8.0 %collective-permute-done.1 = bf16[2064,128]{1,0:T(8,128)(2,1)S(1)} collective-permute-done((bf16[2064,128]{1,0:T(8,128)(2,1)S(1)}, bf16[2064,128]{1,0:T(8,128)(2,1)S(1)}, u32[]{:S(2)}, u32[]{:S(2)}) %collective-permute-start.1) | collective-permute-done | bytes 528416 | tf_op jit(solution)/shard_map/ppermute | solution.py:29
  41.1 0.5 slice.22
  42.3 0.2 fusion.11
  42.5 0.4 fusion.9
  42.9 0.7 copy-done.4
  43.5 3.0 %multiply_reduce_fusion = (f32[256,8]{0,1:T(8,128)S(1)}, f32[256,8,128]{0,2,1:T(8,128)}) fusion(f32[256,8,128]{0,2,1:T(8,128)S(1)} %fusion.9, bf16[256,8,256]{0,2,1:T(8,128)(2,1)S(1)} %fusion.2, bf16[256,8,256]{0,2,1:T(8,128)(2,1)} %copy-done.2, pred[256,256]{1,0:T(8,128)(4,1)S(1)} %fusion.29, bf16[256,1024]{1,0:T(8,128)(2,1)S(1)} %copy-done.4), kind=kOutput, calls=%fused_computation.28 | convolution fusion | flops 404486144 | bytes 4792320 | tf_op jit(solution)/shard_map/hts,shd->thd/dot_general | solution.py:411
  46.6 1.4 multiply_convert_fusion
  48.0 3.5 %fusion.33 = f32[256,2048]{1,0:T(8,128)S(1)} fusion(bf16[256,1024]{0,1:T(8,128)(2,1)S(1)} %bitcast.65, bf16[1024,2048]{1,0:T(8,128)(2,1)} %param.21), kind=kOutput, calls=%fused_computation.63 | convolution fusion | flops 1073741824 | bytes 6815744 | tf_op jit(solution)/shard_map/dot_general | solution.py:429
  51.5 1.0 constant_dynamic-slice_fusion
  52.6 3.0 %collective-permute-done.2 = f32[128,2048]{1,0:T(8,128)} collective-permute-done((f32[128,2048]{1,0:T(8,128)}, f32[128,2048]{1,0:T(8,128)}, u32[]{:S(2)}, u32[]{:S(2)}) %collective-permute-start.2) | collective-permute-done | bytes 1048608 | tf_op jit(solution)/shard_map/ppermute | solution.py:433
  55.6 1.5 fusion.12
  57.1 0.8 copy-done.1
  57.9 0.2 fusion.14
  58.1 0.2 fusion.34
  58.4 0.1 copy.58
  58.6 0.9 fusion.19.x_ref
  59.4 105.0 %shard_map.149 = bf16[128,2048]{1,0:T(8,128)(2,1)} custom-call(bf16[128,2176]{1,0:T(8,128)(2,1)} %fusion.19.x_ref, bf16[1,2048,1024]{2,1,0:T(8,128)(2,1)} %wg_hbm.1, bf16[1,2048,1024]{2,1,0:T(8,128)(2,1)} %wu_hbm.1, bf16[1,1024,2048]{2,1,0:T(8,128)(2,1)} %wd_hbm.1), custom_call_target="tpu_custom_call" | custom-call | flops 25769803776 | bytes 12582912 | tf_op jit(solution)/shard_map/pallas_call | solution.py:330
  164.5 1.9 %copy.89 = bf16[128,2048]{1,0:T(8,128)(2,1)} copy(bf16[128,2048]{1,0:T(8,128)(2,1)} %shard_map.149) | data formatting | bytes 1048576
  (30 shorter events, 0.2 us)
Async XLA Ops:
  0.6 3.3 %copy-start = (bf16[8,128,256]{2,1,0:T(8,128)(2,1)S(1)}, bf16[8,128,256]{2,1,0:T(8,128)(2,1)}, u32[]{:S(2)}) copy-start(bf16[8,128,256]{2,1,0:T(8,128)(2,1)} %param.18) | copy-start | bytes 1572868
  4.0 2.2 %copy-start.3 = (bf16[256,1024]{1,0:T(8,128)(2,1)S(1)}, bf16[256,1024]{1,0:T(8,128)(2,1)}, u32[]{:S(2)}) copy-start(bf16[256,1024]{1,0:T(8,128)(2,1)} %param.16) | copy-start | bytes 1572868
  6.2 1.0 copy-start.2
  7.2 16.1 %collective-permute-start = (bf16[2064,128]{1,0:T(8,128)(2,1)S(1)}, bf16[2064,128]{1,0:T(8,128)(2,1)S(1)}, u32[]{:S(2)}, u32[]{:S(2)}) collective-permute-start(bf16[2064,128]{1,0:T(8,128)(2,1)S(1)} %concatenate.13), channel_id=1, source_target_pairs={{0,2},{2,4},{4,6},{6,8},{8,10},{10,12},{12,14},{1,3},{3,5},{5,7},{... | collective-permute-start | bytes 1585160 | tf_op jit(solution)/shard_map/ppermute | solution.py:29
  25.2 5.6 %copy-start.7 = (s32[256]{0:T(256)S(1)}, s32[256]{0:T(256)}, u32[]{:S(2)}) copy-start(s32[256]{0:T(256)} %param.17) | copy-start | bytes 3076
  25.4 15.7 %collective-permute-start.1 = (bf16[2064,128]{1,0:T(8,128)(2,1)S(1)}, bf16[2064,128]{1,0:T(8,128)(2,1)S(1)}, u32[]{:S(2)}, u32[]{:S(2)}) collective-permute-start(bf16[2064,128]{1,0:T(8,128)(2,1)S(1)} %concatenate.14), channel_id=1, source_target_pairs={{0,4},{2,6},{4,8},{6,10},{8,12},{10,14},{1,5},{3,7},{5,9},{7,11},{... | collective-permute-start | bytes 1585160 | tf_op jit(solution)/shard_map/ppermute | solution.py:29
  42.5 1.0 copy-start.4
  43.5 3.0 %copy-start.10 = (f32[1024]{0:T(1024)S(1)}, f32[1024]{0:T(1024)}, u32[]{:S(2)}) copy-start(f32[1024]{0:T(1024)} %param.19) | copy-start | bytes 12292
  51.5 4.1 %copy-start.5 = (bf16[128,2048]{1,0:T(8,128)(2,1)S(1)}, bf16[128,2048]{1,0:T(8,128)(2,1)}, u32[]{:S(2)}) copy-start(bf16[128,2048]{1,0:T(8,128)(2,1)} %param.20) | copy-start | bytes 1572868
  52.5 5.3 %copy-start.9 = (f32[2048]{0:T(1024)S(1)}, f32[2048]{0:T(1024)}, u32[]{:S(2)}) copy-start(f32[2048]{0:T(1024)} %param.22) | copy-start | bytes 24580
  52.5 3.0 %collective-permute-start.2 = (f32[128,2048]{1,0:T(8,128)}, f32[128,2048]{1,0:T(8,128)}, u32[]{:S(2)}, u32[]{:S(2)}) collective-permute-start(f32[128,2048]{1,0:T(8,128)} %constant_dynamic-slice_fusion), channel_id=1, source_target_pairs={{0,1},{1,0},{2,3},{3,2},{4,5},{5,4},{6,7},{7,6},{8,9},{9,8},{10,11... | collective-permute-start | bytes 3145736 | tf_op jit(solution)/shard_map/ppermute | solution.py:433
  52.5 5.5 %copy-start.6 = (bf16[2048,16]{0,1:T(8,128)(2,1)S(1)}, bf16[2048,16]{0,1:T(8,128)(2,1)}, u32[]{:S(2)}) copy-start(bf16[2048,16]{0,1:T(8,128)(2,1)} %param.23) | copy-start | bytes 196612
  52.5 5.8 %copy-start.8 = (s32[128,8]{0,1:T(8,128)S(1)}, s32[128,8]{0,1:T(8,128)}, u32[]{:S(2)}) copy-start(s32[128,8]{0,1:T(8,128)} %param.27) | copy-start | bytes 12292
  57.1 0.8 copy-start.1

commit v3 on v2

--- a/solution.py
+++ b/solution.py
@@ -8,44 +8,6 @@
 from jax.sharding import PartitionSpec as P
 
 
-def carried_in(last_seg, local_state, token_count):
-    blocks = lax.axis_size("seq")
-    longest = token_count * blocks // 3
-    reach = min(blocks - 1, max(1, (longest - 2) // token_count + 1))
-    state_rows = local_state.shape[0] * local_state.shape[1]
-    width = local_state.shape[2]
-    before = None
-    carried = None
-    window = local_state
-    span = 1
-    covered = 0
-    while covered < reach:
-        packet = jnp.concatenate(
-            [
-                window.reshape(state_rows, width).astype(jnp.bfloat16),
-                jnp.full((16, width), last_seg, jnp.bfloat16),
-            ]
-        )
-        arrived = lax.ppermute(packet, "seq", [(i, i + span) for i in range(blocks - span)])
-        shifted = arrived[:state_rows].astype(jnp.float32).reshape(local_state.shape)
-        seg = arrived[state_rows, 0].astype(jnp.int32)
-        if carried is None:
-            before, carried = seg, shifted
-        else:
-            carried = carried + jnp.where(seg == before, shifted, 0.0)
-        covered += span
-        if covered < reach:
-            window = window + jnp.where(seg == last_seg, shifted, 0.0)
-        span *= 2
-    return before, carried
-
-
-def features_of(inputs, feature_map, head_count, head_dim):
-    grouped = inputs.reshape(inputs.shape[0], head_count, head_dim)
-    projected = jnp.einsum("thd,hdf->thf", grouped, feature_map, preferred_element_type=jnp.float32)
-    return (jax.nn.elu(projected) + 1.0).astype(jnp.bfloat16)
-
-
 def run_expert(rows, gate, w_gate, w_up, w_down):
     gate_pre = jnp.dot(rows, w_gate, preferred_element_type=jnp.float32)
     up_pre = jnp.dot(rows, w_up, preferred_element_type=jnp.float32)
@@ -55,6 +17,234 @@
 
 
 MESH = pl.DeviceIdType.MESH
+
+
+def spans_of(token_count, blocks):
+    longest = token_count * blocks // 3
+    reach = min(blocks - 1, max(1, (longest - 2) // token_count + 1))
+    spans = []
+    while sum(spans) < reach:
+        spans.append(2 ** len(spans))
+    return spans
+
+
+def attn_kernel(
+    blocks,
+    spans,
+    q_ref,
+    k_ref,
+    v_ref,
+    seg_col,
+    seg_row,
+    map_ref,
+    gain_ref,
+    out_ref,
+    key_feat,
+    query_feat,
+    window,
+    carried,
+    within,
+    outbox,
+    inbox,
+    seg_out,
+    seg_in,
+    send_sem,
+    recv_sem,
+    seg_send,
+    seg_recv,
+):
+    tokens = q_ref.shape[0]
+    heads, dim, _ = map_ref.shape
+    place = lax.axis_index("seq")
+    f32, bf16 = jnp.float32, jnp.bfloat16
+
+    barrier = pltpu.get_barrier_semaphore()
+    for span in spans:
+        for shift in (span, blocks - span):
+            other = (place + shift) % blocks
+            pl.semaphore_signal(barrier, inc=1, device_id={"seq": other}, device_id_type=MESH)
+    pl.semaphore_wait(barrier, 2 * len(spans))
+
+    def packet(i, h):
+        return pltpu.make_async_remote_copy(
+            src_ref=outbox.at[i, h],
+            dst_ref=inbox.at[i, h],
+            send_sem=send_sem.at[i, h],
+            recv_sem=recv_sem.at[i, h],
+            device_id={"seq": place + spans[i]},
+            device_id_type=MESH,
+        )
+
+    def note(i):
+        return pltpu.make_async_remote_copy(
+            src_ref=seg_out,
+            dst_ref=seg_in.at[i],
+            send_sem=seg_send.at[i],
+            recv_sem=seg_recv.at[i],
+            device_id={"seq": place + spans[i]},
+            device_id_type=MESH,
+        )
+
+    last = seg_col[tokens - 1 : tokens, :]
+    seg_out[...] = jnp.broadcast_to(last.astype(f32), seg_out.shape)
+    for i, span in enumerate(spans):
+
+        @pl.when(place + span < blocks)
+        def _tell(i=i):
+            note(i).start()
+
+        @pl.when(place < span)
+        def _none(i=i):
+            seg_in[i] = jnp.full(seg_in.shape[1:], -1.0, f32)
+            inbox[i] = jnp.zeros(inbox.shape[1:], bf16)
+
+    def features(x, h):
+        projected = jnp.dot(x, map_ref[h], preferred_element_type=f32)
+        return jnp.where(projected > 0, projected + 1.0, jnp.exp(jnp.minimum(projected, 0.0))).astype(
+            bf16
+        )
+
+    def lanes(h):
+        return pl.ds(pl.multiple_of(h * dim, dim), dim)
+
+    def send(i, h):
+        outbox[i, h] = window[h].astype(bf16)
+
+        @pl.when(place + spans[i] < blocks)
+        def _go():
+            packet(i, h).start()
+
+    tail = seg_col[...] == last
+
+    def key_step(h, carry):
+        feat = features(k_ref[:, lanes(h)], h)
+        key_feat[h] = feat
+        tail_values = jnp.where(tail, v_ref[:, lanes(h)].astype(f32), 0.0).astype(bf16)
+        window[h] = lax.dot_general(
+            feat, tail_values, (((0,), (0,)), ((), ())), preferred_element_type=f32
+        )
+        send(0, h)
+        return carry
+
+    lax.fori_loop(0, heads, key_step, 0)
+    for i, span in enumerate(spans):
+
+        @pl.when(place >= span)
+        def _told(i=i):
+            note(i).wait_recv()
+
+    last_f = last.astype(f32)
+    before = seg_in[0, 0:1, 0:1]
+    reached = seg_col[...].astype(f32) == before
+    row = lax.broadcasted_iota(jnp.int32, (tokens, tokens), 0)
+    col = lax.broadcasted_iota(jnp.int32, (tokens, tokens), 1)
+    allowed = (col <= row) & (seg_col[...] == seg_row[...])
+
+    def take(i, h):
+        @pl.when(place >= spans[i])
+        def _arrived():
+            packet(i, h).wait_recv()
+
+        shifted = inbox[i, h].astype(f32)
+        seg = seg_in[i, 0:1, 0:1]
+        if i == 0:
+            carried[h] = shifted
+        else:
+            carried[h] = carried[h] + jnp.where(seg == before, shifted, 0.0)
+        if i + 1 < len(spans):
+            window[h] = window[h] + jnp.where(seg == last_f, shifted, 0.0)
+            send(i + 1, h)
+
+    def finish(h):
+        far = jnp.dot(query_feat[h], carried[h].astype(bf16), preferred_element_type=f32)
+        mixed = within[:, lanes(h)] + jnp.where(reached, far, 0.0)
+        scale = lax.rsqrt(jnp.mean(mixed * mixed, axis=1, keepdims=True) + 1e-06)
+        out_ref[:, lanes(h)] = (mixed * scale * gain_ref[:, lanes(h)]).astype(bf16)
+
+    def query_step(h, carry):
+        feat = features(q_ref[:, lanes(h)], h)
+        query_feat[h] = feat
+        scores = lax.dot_general(
+            feat, key_feat[h], (((1,), (1,)), ((), ())), preferred_element_type=f32
+        )
+        weights = jnp.where(allowed, scores, 0.0).astype(bf16)
+        within[:, lanes(h)] = jnp.dot(weights, v_ref[:, lanes(h)], preferred_element_type=f32)
+        take(0, h)
+        return carry
+
+    lax.fori_loop(0, heads, query_step, 0)
+    for i in range(1, len(spans)):
+
+        def later_step(h, carry, i=i):
+            take(i, h)
+            if i == len(spans) - 1:
+                finish(h)
+            return carry
+
+        lax.fori_loop(0, heads, later_step, 0)
+    if len(spans) == 1:
+
+        def last_step(h, carry):
+            finish(h)
+            return carry
+
+        lax.fori_loop(0, heads, last_step, 0)
+
+    for i, span in enumerate(spans):
+
+        @pl.when(place + span < blocks)
+        def _sent(i=i):
+            note(i).wait_send()
+
+            def done_step(h, carry):
+                packet(i, h).wait_send()
+                return carry
+
+            lax.fori_loop(0, heads, done_step, 0)
+
+
+def attention(query_proj, key_proj, value_proj, segment_ids, feature_map, head_gain):
+    tokens = query_proj.shape[0]
+    heads, dim, feat = feature_map.shape
+    blocks = lax.axis_size("seq")
+    spans = spans_of(tokens, blocks)
+    count = len(spans)
+    dma = pltpu.SemaphoreType.DMA
+    f32, bf16 = jnp.float32, jnp.bfloat16
+    return pl.pallas_call(
+        functools.partial(attn_kernel, blocks, spans),
+        out_shape=jax.ShapeDtypeStruct((tokens, heads * dim), bf16),
+        in_specs=[pl.BlockSpec(memory_space=pltpu.VMEM)] * 7,
+        out_specs=pl.BlockSpec(memory_space=pltpu.VMEM),
+        scratch_shapes=[
+            pltpu.VMEM((heads, tokens, feat), bf16),
+            pltpu.VMEM((heads, tokens, feat), bf16),
+            pltpu.VMEM((heads, feat, dim), f32),
+            pltpu.VMEM((heads, feat, dim), f32),
+            pltpu.VMEM((tokens, heads * dim), f32),
+            pltpu.VMEM((count, heads, feat, dim), bf16),
+            pltpu.VMEM((count, heads, feat, dim), bf16),
+            pltpu.VMEM((8, 128), f32),
+            pltpu.VMEM((count, 8, 128), f32),
+            dma((count, heads)),
+            dma((count, heads)),
+            dma((count,)),
+            dma((count,)),
+        ],
+        compiler_params=pltpu.CompilerParams(
+            collective_id=1, has_side_effects=True, vmem_limit_bytes=32 * 1024 * 1024
+        ),
+    )(
+        query_proj,
+        key_proj,
+        value_proj,
+        segment_ids.reshape(tokens, 1),
+        segment_ids.reshape(1, tokens),
+        feature_map,
+        head_gain.reshape(1, heads * dim),
+    )
+
+
 TILE = 256
 VMEM_MOST = 63 * 1024 * 1024
 
@@ -387,42 +577,7 @@
     w_down,
     expert_ids,
 ):
-    token_count = query_proj.shape[0]
-    head_count = feature_map.shape[0]
-    head_dim = feature_map.shape[1]
-    query_feat = features_of(query_proj, feature_map, head_count, head_dim)
-    key_feat = features_of(key_proj, feature_map, head_count, head_dim)
-    values = value_proj.reshape(token_count, head_count, head_dim)
-    last_seg = segment_ids[token_count - 1]
-    tail_mask = (segment_ids == last_seg).astype(jnp.bfloat16)
-    local_state = jnp.einsum(
-        "thf,thd->hfd",
-        key_feat * tail_mask[:, None, None],
-        values,
-        preferred_element_type=jnp.float32,
-    )
-    seg_before, state_before = carried_in(last_seg, local_state, token_count)
-    scores = jnp.einsum("thf,shf->hts", query_feat, key_feat, preferred_element_type=jnp.float32)
-    positions = lax.iota(jnp.int32, token_count)
-    allowed = (positions[None, :] <= positions[:, None]) & (
-        segment_ids[None, :] == segment_ids[:, None]
-    )
-    block_weights = jnp.where(allowed[None], scores, 0.0).astype(jnp.bfloat16)
-    within = jnp.einsum("hts,shd->thd", block_weights, values, preferred_element_type=jnp.float32)
-    carried = jnp.einsum(
-        "thf,hfd->thd",
-        query_feat,
-        state_before.astype(jnp.bfloat16),
-        preferred_element_type=jnp.float32,
-    )
-    carry_mask = (segment_ids == seg_before).astype(jnp.float32)
-    mixed = within + carry_mask[:, None, None] * carried
-    scale = lax.rsqrt(jnp.mean(mixed * mixed, axis=2, keepdims=True) + 1e-06)
-    attn_heads = (
-        (mixed * scale * head_gain.reshape(head_count, head_dim))
-        .reshape(token_count, head_count * head_dim)
-        .astype(jnp.bfloat16)
-    )
+    attn_heads = attention(query_proj, key_proj, value_proj, segment_ids, feature_map, head_gain)
     row_count = residual.shape[0]
     head_place = lax.axis_index("head")
     head_devs = lax.axis_size("head")

time: 167 us -> 154 us (0.922)
  Pallas kernels: 105 us -> 133 us
  waiting for transfers between devices: 22.3 us -> 3 us
  starting transfers between devices: 10.3 us -> 0.01 us
  matrix products: 11.9 us -> 3.67 us
  other arithmetic: 5.91 us -> 2.79 us
  between operations: 3.54 us -> 0.79 us
  local copies, waits for them, and re-layouts: 7.44 us -> 9.44 us
    pallas_call x0 -> x1, Pallas kernels: none -> 21.8 us  [attention(): pl.pallas_call(functools.partial(attn_kernel, blocks, spans), out_shape=j...]
    ppermute x2 -> x0, waiting for transfers between devices: 19.3 us -> none  [carried_in(): lax.ppermute(packet, 'seq', [(i, i + span) for i in range(blocks - span)])]
    ppermute x2 -> x0, starting transfers between devices: 10.3 us -> none  [carried_in(): lax.ppermute(packet, 'seq', [(i, i + span) for i in range(blocks - span)])]
    dot_general x5 -> x0, matrix products: 8.17 us -> none  [the longest x2 4.36 us: features_of(): jnp.einsum('thd,hdf->thf', grouped, feature_map, preferred_element_type=j...]
    pallas_call x1, Pallas kernels: 105 us -> 112 us  [moe(): pl.pallas_call(functools.partial(moe_kernel, count, folded, experts), out...]
    unnamed x23 -> x21, local copies, waits for them, and re-layouts: 3.86 us -> 7.43 us
    convert_element_type x5 -> x0, other arithmetic: 3.07 us -> none  [the longest x1 1.43 us: shards(): attn_heads = (mixed * scale * head_gain.reshape(head_count, head_dim)).re...]
    slice x3 -> x0, local copies, waits for them, and re-layouts: 2.34 us -> none  [the longest x1 1.32 us: shards(): last_seg = segment_ids[token_count - 1]]
  transfers between devices with their start and end apart: 3 -> 1, of which waited for: 3 -> 1; matrix products, arithmetic and copies ran while one was open for 1% -> 0% of each run, Pallas kernels for 0% -> 0%
where the time goes in v3:
time: 154 us; the launch traced here: 153 us
  Pallas kernels  133 us (86%)
  local copies, waits for them, and re-layouts  9.44 us (6%)
  matrix products  3.67 us (2%)
  waiting for transfers between devices  3 us (2%)
  other arithmetic  2.79 us (2%)
    pallas_call x1, Pallas kernels, moe(): pl.pallas_call(functools.partial(moe_kernel, count, folded, experts), out...  112 us
    pallas_call x1, Pallas kernels, attention(): pl.pallas_call(functools.partial(attn_kernel, blocks, spans), out_shape=j...  21.8 us
    unnamed x21, local copies, waits for them, and re-layouts  7.43 us
    dot_general x1, matrix products, shards(): sums = jnp.dot(attn_heads, out_weight, preferred_element_type=jnp.float32)  3.44 us
  transfers between devices with their start and end apart: 1, of which 1 were waited for; matrix products, arithmetic and copies ran while one was open for 0% of the time, Pallas kernels for 0%

profile of v3, /device:TPU:0, one launch (start us, length us, event | category | flops | bytes accessed | tf_op | source)
XLA Modules:
  0.0 153.2 jit_solution(356479790428601364)
XLA Ops:
  0.6 0.0 copy-start
  0.7 0.8 copy.25.seg_col
  1.5 0.0 copy-start.1
  1.5 1.0 copy-done.1
  2.6 0.0 copy-start.2
  2.6 1.0 copy-done.2
  3.6 0.0 copy-start.3
  3.6 1.0 copy-done.3
  4.6 0.0 copy-start.4
  4.6 1.0 copy-done.4
  5.7 0.0 copy-start.5
  5.7 0.7 copy-done.5
  6.4 0.0 copy-start.6
  6.4 0.7 copy-done.6
  7.0 21.8 %shard_map.149 = bf16[256,1024]{1,0:T(8,128)(2,1)S(1)} custom-call(bf16[256,1024]{1,0:T(8,128)(2,1)S(1)} %copy-done.1, bf16[256,1024]{1,0:T(8,128)(2,1)S(1)} %copy-done.2, bf16[256,1024]{1,0:T(8,128)(2,1)S(1)} %copy-done.3, s32[256,1]{1,0:T(8,128)S(1)} %copy.25.seg_col, s32[1,256]{1,0:T(1,128)S(1)} %bitcast.8, bf16[8,128,256]{2,1,0:T(8,128)(2,1)S(1)} %copy-done.4, ...), custom_call_target="tpu_custom_call" | custom-call | tf_op jit(solution)/shard_map/pallas_call | solution.py:214
  28.8 3.4 %fusion.6 = f32[256,2048]{1,0:T(8,128)S(1)} fusion(bf16[256,1024]{1,0:T(8,128)(2,1)S(1)} %shard_map.149, bf16[1024,2048]{1,0:T(8,128)(2,1)} %param.21), kind=kOutput, calls=%fused_computation.21 | convolution fusion | flops 1073741824 | bytes 6815744 | tf_op jit(solution)/shard_map/dot_general | solution.py:584
  32.3 1.1 constant_dynamic-slice_fusion
  33.3 0.0 copy-start.9
  33.3 0.0 collective-permute-start
  33.4 3.0 %collective-permute-done = f32[128,2048]{1,0:T(8,128)} collective-permute-done((f32[128,2048]{1,0:T(8,128)}, f32[128,2048]{1,0:T(8,128)}, u32[]{:S(2)}, u32[]{:S(2)}) %collective-permute-start) | collective-permute-done | bytes 1048608 | tf_op jit(solution)/shard_map/ppermute | solution.py:588
  36.4 1.6 %fusion.1 = (f32[128]{0:T(128)S(1)}, bf16[128,2048]{1,0:T(8,128)(2,1)S(1)}) fusion(f32[128,2048]{1,0:T(8,128)} %collective-permute-done, f32[256,2048]{1,0:T(8,128)S(1)} %fusion.6, s32[]{:T(128)S(6)} %select_n.21, bf16[128,2048]{1,0:T(8,128)(2,1)} %param.20), kind=kLoop, calls=%fused_computation.4 | loop fusion | flops 1834880 | bytes 3146244 | tf_op jit(solution)/shard_map/reduce_sum | solution.py:597
  38.0 0.0 copy-start.7
  38.0 0.0 copy-done.9
  38.0 0.2 fusion.3
  38.2 0.0 copy-done
  38.2 0.2 fusion.7
  38.5 0.0 copy-done.8
  38.6 0.1 copy.26
  38.7 0.8 fusion.4.x_ref
  39.6 111.7 %shard_map.150 = bf16[128,2048]{1,0:T(8,128)(2,1)} custom-call(bf16[128,2176]{1,0:T(8,128)(2,1)} %fusion.4.x_ref, bf16[1,2048,1024]{2,1,0:T(8,128)(2,1)} %wg_hbm.1, bf16[1,2048,1024]{2,1,0:T(8,128)(2,1)} %wu_hbm.1, bf16[1,1024,2048]{2,1,0:T(8,128)(2,1)} %wd_hbm.1), custom_call_target="tpu_custom_call" | custom-call | flops 25769803776 | bytes 12582912 | tf_op jit(solution)/shard_map/pallas_call | solution.py:520
  151.3 0.0 copy-done.7
  151.3 1.9 %copy.28 = bf16[128,2048]{1,0:T(8,128)(2,1)} copy(bf16[128,2048]{1,0:T(8,128)(2,1)} %shard_map.150) | data formatting | bytes 1048576
  (8 shorter events, 0.1 us)
Async XLA Ops:
  0.6 37.6 %copy-start = (bf16[2048,16]{0,1:T(8,128)(2,1)S(1)}, bf16[2048,16]{0,1:T(8,128)(2,1)}, u32[]{:S(2)}) copy-start(bf16[2048,16]{0,1:T(8,128)(2,1)} %param.23) | copy-start | bytes 196612
  1.5 1.0 copy-start.1
  2.6 1.0 copy-start.2
  3.6 1.0 copy-start.3
  4.6 1.0 copy-start.4
  5.7 0.7 copy-start.5
  6.4 0.7 copy-start.6
  33.3 4.7 %copy-start.9 = (f32[2048]{0:T(1024)S(1)}, f32[2048]{0:T(1024)}, u32[]{:S(2)}) copy-start(f32[2048]{0:T(1024)} %param.22) | copy-start | bytes 24580
  33.3 3.0 %collective-permute-start = (f32[128,2048]{1,0:T(8,128)}, f32[128,2048]{1,0:T(8,128)}, u32[]{:S(2)}, u32[]{:S(2)}) collective-permute-start(f32[128,2048]{1,0:T(8,128)} %constant_dynamic-slice_fusion), channel_id=1, source_target_pairs={{0,1},{1,0},{2,3},{3,2},{4,5},{5,4},{6,7},{7,6},{8,9},{9,8},{10,11... | collective-permute-start | bytes 3145736 | tf_op jit(solution)/shard_map/ppermute | solution.py:588
  33.4 5.1 %copy-start.8 = (s32[128,8]{0,1:T(8,128)S(1)}, s32[128,8]{0,1:T(8,128)}, u32[]{:S(2)}) copy-start(s32[128,8]{0,1:T(8,128)} %param.27) | copy-start | bytes 12292
  38.0 113.3 %copy-start.7 = (bf16[128,2048]{1,0:T(8,128)(2,1)}, bf16[128,2048]{1,0:T(8,128)(2,1)S(1)}, u32[]{:S(2)}) copy-start(bf16[128,2048]{1,0:T(8,128)(2,1)S(1)} %get-tuple-element.8) | copy-start | bytes 1572868

commit v4 on v3

--- a/solution.py
+++ b/solution.py
@@ -31,14 +31,19 @@
 def attn_kernel(
     blocks,
     spans,
+    q_hbm,
+    k_hbm,
+    v_hbm,
+    seg_col,
+    seg_row,
+    map_hbm,
+    gain_ref,
+    out_ref,
     q_ref,
     k_ref,
     v_ref,
-    seg_col,
-    seg_row,
     map_ref,
-    gain_ref,
-    out_ref,
+    load_sem,
     key_feat,
     query_feat,
     window,
@@ -58,6 +63,13 @@
     place = lax.axis_index("seq")
     f32, bf16 = jnp.float32, jnp.bfloat16
 
+    sources = ((k_hbm, k_ref), (map_hbm, map_ref), (v_hbm, v_ref), (q_hbm, q_ref))
+    loads = [
+        pltpu.make_async_copy(src, dst, load_sem.at[i]) for i, (src, dst) in enumerate(sources)
+    ]
+    for load in loads:
+        load.start()
+
     barrier = pltpu.get_barrier_semaphore()
     for span in spans:
         for shift in (span, blocks - span):
@@ -126,7 +138,10 @@
         send(0, h)
         return carry
 
+    for load in loads[:3]:
+        load.wait()
     lax.fori_loop(0, heads, key_step, 0)
+    loads[3].wait()
     for i, span in enumerate(spans):
 
         @pl.when(place >= span)
@@ -211,12 +226,19 @@
     count = len(spans)
     dma = pltpu.SemaphoreType.DMA
     f32, bf16 = jnp.float32, jnp.bfloat16
+    in_any = pl.BlockSpec(memory_space=pl.ANY)
+    in_vmem = pl.BlockSpec(memory_space=pltpu.VMEM)
     return pl.pallas_call(
         functools.partial(attn_kernel, blocks, spans),
         out_shape=jax.ShapeDtypeStruct((tokens, heads * dim), bf16),
-        in_specs=[pl.BlockSpec(memory_space=pltpu.VMEM)] * 7,
+        in_specs=[in_any, in_any, in_any, in_vmem, in_vmem, in_any, in_vmem],
         out_specs=pl.BlockSpec(memory_space=pltpu.VMEM),
         scratch_shapes=[
+            pltpu.VMEM(query_proj.shape, bf16),
+            pltpu.VMEM(key_proj.shape, bf16),
+            pltpu.VMEM(value_proj.shape, bf16),
+            pltpu.VMEM(feature_map.shape, bf16),
+            dma((4,)),
             pltpu.VMEM((heads, tokens, feat), bf16),
             pltpu.VMEM((heads, tokens, feat), bf16),
             pltpu.VMEM((heads, feat, dim), f32),
@@ -268,6 +290,7 @@
     count,
     folded,
     experts,
+    taken_most,
     x_ref,
     wg_hbm,
     wu_hbm,
@@ -281,6 +304,7 @@
     wu,
     wd,
     act,
+    packed,
     load_sem,
     ag_send,
     ag_recv,
@@ -378,29 +402,67 @@
         )
 
     def compute(first_slot, blocks):
-        low = spot(first_slot) * 2 * rows
-        tall = blocks * 2 * rows
+        pair_rows = 2 * rows
         expert = lax.axis_index("seq") * 2 + core
-        taken = pl.ds(low, tall)
-        extra = rows_buf[taken, width:].astype(jnp.float32)
-        lane = lax.broadcasted_iota(jnp.int32, extra.shape, 1)
-        mine = (lane == expert) | (lane == expert + experts)
-        gate = jnp.sum(jnp.where(mine, extra, 0.0), axis=1, keepdims=True)
+        f32, bf16 = jnp.float32, jnp.bfloat16
+        row = lax.broadcasted_iota(jnp.int32, (pair_rows, pair_rows), 0)
+        col = lax.broadcasted_iota(jnp.int32, (pair_rows, pair_rows), 1)
+        earlier_row = jnp.where(row < col, 1.0, 0.0).astype(bf16)
+        earlier_col = jnp.where(col < row, 1.0, 0.0).astype(bf16)
+        slot_down = lax.broadcasted_iota(jnp.int32, (taken_most, pair_rows), 0).astype(f32)
+        slot_across = lax.broadcasted_iota(jnp.int32, (pair_rows, taken_most), 1).astype(f32)
+        ones = jnp.ones((8, padded - width), bf16)
+        gates, backs, places = [], [], []
+        for j in range(blocks):
+            taken = pl.ds(spot(first_slot) * pair_rows + j * pair_rows, pair_rows)
+            extra = rows_buf[taken, width:].astype(f32)
+            lane = lax.broadcasted_iota(jnp.int32, extra.shape, 1)
+            mine = (lane == expert) | (lane == expert + experts)
+            gate = jnp.sum(jnp.where(mine, extra, 0.0), axis=1, keepdims=True)
+            named = jnp.where((lane == expert) & (gate > 0), 1.0, 0.0)
+            named_col = jnp.sum(named, axis=1, keepdims=True)
+            named = named.astype(bf16)
+            named_row = lax.dot_general(
+                ones, named, (((1,), (1,)), ((), ())), preferred_element_type=f32
+            )
+            ahead_row = jnp.dot(named_row.astype(bf16), earlier_row, preferred_element_type=f32)
+            ahead_col = jnp.sum(
+                jnp.dot(earlier_col, named, preferred_element_type=f32), axis=1, keepdims=True
+            )
+            pick = jnp.where((slot_down == ahead_row[0:1]) & (named_row[0:1] > 0), 1.0, 0.0)
+            back = jnp.where((slot_across == ahead_col) & (named_col > 0), 1.0, 0.0)
+            pick = pick.astype(bf16)
+            gates.append(gate)
+            backs.append(back.astype(bf16))
+            places.append(taken)
+
+            def pack_step(t, carry, j=j, pick=pick, taken=taken):
+                cols = pl.ds(pl.multiple_of(t * TILE, TILE), TILE)
+                packed[j * taken_most : (j + 1) * taken_most, cols] = jnp.dot(
+                    pick, rows_buf[taken, cols], preferred_element_type=f32
+                ).astype(bf16)
+                return carry
+
+            lax.fori_loop(0, width // TILE, pack_step, 0)
+        tall = blocks * taken_most
 
         def up_step(t, carry):
             cols = pl.ds(pl.multiple_of(t * TILE, TILE), TILE)
-            x = rows_buf[taken, :width]
-            gate_pre = jnp.dot(x, wg[:, cols], preferred_element_type=jnp.float32)
-            up_pre = jnp.dot(x, wu[:, cols], preferred_element_type=jnp.float32)
-            act[:tall, cols] = (gate_pre * jax.nn.sigmoid(gate_pre) * up_pre).astype(jnp.bfloat16)
+            x = packed[:tall, :]
+            gate_pre = jnp.dot(x, wg[:, cols], preferred_element_type=f32)
+            up_pre = jnp.dot(x, wu[:, cols], preferred_element_type=f32)
+            act[:tall, cols] = (gate_pre * jax.nn.sigmoid(gate_pre) * up_pre).astype(bf16)
             return carry
 
         lax.fori_loop(0, wg.shape[1] // TILE, up_step, 0)
 
         def down_step(t, carry):
             cols = pl.ds(pl.multiple_of(t * TILE, TILE), TILE)
-            answer = jnp.dot(act[:tall, :], wd[:, cols], preferred_element_type=jnp.float32)
-            part[taken, cols] = (answer * gate).astype(jnp.bfloat16)
+            answer = jnp.dot(act[:tall, :], wd[:, cols], preferred_element_type=f32).astype(bf16)
+            for j in range(blocks):
+                own = answer[j * taken_most : (j + 1) * taken_most]
+                spread = jnp.dot(backs[j], own, preferred_element_type=f32)
+                part[places[j], cols] = (spread * gates[j]).astype(bf16)
             return carry
 
         lax.fori_loop(0, width // TILE, down_step, 0)
@@ -493,7 +555,12 @@
             copy.wait_send()
 
 
-def moe_scratch(count, rows, padded, width, hidden):
+def taken_bound(rows, top_count, experts):
+    capacity = rows * top_count * 5 // (4 * experts)
+    return -(-2 * capacity // 16) * 16
+
+
+def moe_scratch(count, rows, padded, width, hidden, taken_most):
     half = rows // 2
     far = count // 2
     tall = count * 2 * rows
@@ -506,19 +573,21 @@
         ((width, hidden), bf16),
         ((width, hidden), bf16),
         ((hidden, width), bf16),
-        ((4 * rows, hidden), bf16),
+        ((2 * taken_most, hidden), bf16),
+        ((2 * taken_most, width), bf16),
     ]
 
 
-def moe(rows_in, width, experts, w_gate, w_up, w_down, folded):
+def moe(rows_in, width, experts, top_count, w_gate, w_up, w_down, folded):
     count = lax.axis_size("seq")
     rows, padded = rows_in.shape
     far = count // 2
     dma = pltpu.SemaphoreType.DMA
-    scratch = moe_scratch(count, rows, padded, width, w_gate.shape[2])
+    taken_most = taken_bound(rows, top_count, experts)
+    scratch = moe_scratch(count, rows, padded, width, w_gate.shape[2], taken_most)
     tall = count * 2 * rows
     return pl.pallas_call(
-        functools.partial(moe_kernel, count, folded, experts),
+        functools.partial(moe_kernel, count, folded, experts, taken_most),
         out_shape=jax.ShapeDtypeStruct((rows, width), jnp.bfloat16),
         in_specs=[pl.BlockSpec(memory_space=pltpu.VMEM)]
         + [pl.BlockSpec(memory_space=pl.ANY)] * 3,
@@ -546,13 +615,13 @@
     )(rows_in, w_gate, w_up, w_down)
 
 
-def moe_fits(count, heads, rows, padded, width, w_gate):
+def moe_fits(count, heads, rows, padded, width, w_gate, taken_most):
     if heads != 2 or count < 4 or count % 2 or w_gate.shape[0] != 1:
         return False
     if rows % 32 or width % TILE or w_gate.shape[2] % TILE:
         return False
     need = 0
-    for shape, _ in moe_scratch(count, rows, padded, width, w_gate.shape[2]):
+    for shape, _ in moe_scratch(count, rows, padded, width, w_gate.shape[2], taken_most):
         size = 2
         for extent in shape:
             size *= extent
@@ -610,9 +679,13 @@
     lanes = -(-2 * expert_count // 128) * 128
     extra = jnp.concatenate([coarse, dense_gates - coarse], axis=1).astype(jnp.bfloat16)
     extra = jnp.pad(extra, ((0, 0), (0, lanes - 2 * expert_count)))
-    if moe_fits(lax.axis_size("seq"), head_devs, row_count, model_width + lanes, model_width, w_gate):
+    top_count = expert_ids.shape[1]
+    taken_most = taken_bound(row_count, top_count, expert_count)
+    if moe_fits(
+        lax.axis_size("seq"), head_devs, row_count, model_width + lanes, model_width, w_gate, taken_most
+    ):
         rows_in = jnp.concatenate([normed, extra], axis=1)
-        expert_sum = moe(rows_in, model_width, expert_count, w_gate, w_up, w_down, folded)
+        expert_sum = moe(rows_in, model_width, expert_count, top_count, w_gate, w_up, w_down, folded)
         return (hidden, expert_sum)
     spread = ("seq", "head")
     all_rows = lax.all_gather(normed, spread, axis=0, tiled=True)

time: 154 us -> 166 us (1.078)
  Pallas kernels: 133 us -> 146 us
    pallas_call x1, Pallas kernels: 112 us -> 124 us  [moe(): pl.pallas_call(functools.partial(moe_kernel, count, folded, experts, take...]
where the time goes in v4:
time: 166 us; the launch traced here: 165 us
  Pallas kernels  146 us (88%)
  local copies, waits for them, and re-layouts  9.44 us (6%)
  matrix products  3.67 us (2%)
  waiting for transfers between devices  3 us (2%)
  other arithmetic  2.79 us (2%)
    pallas_call x1, Pallas kernels, moe(): pl.pallas_call(functools.partial(moe_kernel, count, folded, experts, take...  124 us
    pallas_call x1, Pallas kernels, attention(): pl.pallas_call(functools.partial(attn_kernel, blocks, spans), out_shape=j...  22 us
    unnamed x21, local copies, waits for them, and re-layouts  7.43 us
    dot_general x1, matrix products, shards(): sums = jnp.dot(attn_heads, out_weight, preferred_element_type=jnp.float32)  3.44 us
  transfers between devices with their start and end apart: 1, of which 1 were waited for; matrix products, arithmetic and copies ran while one was open for 0% of the time, Pallas kernels for 0%

profile of v4, /device:TPU:0, one launch (start us, length us, event | category | flops | bytes accessed | tf_op | source)
XLA Modules:
  0.0 165.2 jit_solution(5111633588919556121)
XLA Ops:
  0.6 0.0 copy-start
  0.7 0.8 copy.25.seg_col
  1.5 0.0 copy-start.1
  1.5 1.0 copy-done.1
  2.6 0.0 copy-start.2
  2.6 1.0 copy-done.2
  3.6 0.0 copy-start.3
  3.6 1.0 copy-done.3
  4.6 0.0 copy-start.4
  4.6 1.0 copy-done.4
  5.7 0.0 copy-start.5
  5.7 0.7 copy-done.5
  6.4 0.0 copy-start.6
  6.4 0.7 copy-done.6
  7.0 22.0 %shard_map.149 = bf16[256,1024]{1,0:T(8,128)(2,1)S(1)} custom-call(bf16[256,1024]{1,0:T(8,128)(2,1)S(1)} %copy-done.1, bf16[256,1024]{1,0:T(8,128)(2,1)S(1)} %copy-done.2, bf16[256,1024]{1,0:T(8,128)(2,1)S(1)} %copy-done.3, s32[256,1]{1,0:T(8,128)S(1)} %copy.25.seg_col, s32[1,256]{1,0:T(1,128)S(1)} %bitcast.8, bf16[8,128,256]{2,1,0:T(8,128)(2,1)S(1)} %copy-done.4, ...), custom_call_target="tpu_custom_call" | custom-call | tf_op jit(solution)/shard_map/pallas_call | solution.py:231
  29.0 3.4 %fusion.6 = f32[256,2048]{1,0:T(8,128)S(1)} fusion(bf16[256,1024]{1,0:T(8,128)(2,1)S(1)} %shard_map.149, bf16[1024,2048]{1,0:T(8,128)(2,1)} %param.21), kind=kOutput, calls=%fused_computation.21 | convolution fusion | flops 1073741824 | bytes 6815744 | tf_op jit(solution)/shard_map/dot_general | solution.py:653
  32.5 1.1 constant_dynamic-slice_fusion
  33.5 0.0 copy-start.9
  33.5 0.0 collective-permute-start
  33.5 3.0 %collective-permute-done = f32[128,2048]{1,0:T(8,128)} collective-permute-done((f32[128,2048]{1,0:T(8,128)}, f32[128,2048]{1,0:T(8,128)}, u32[]{:S(2)}, u32[]{:S(2)}) %collective-permute-start) | collective-permute-done | bytes 1048608 | tf_op jit(solution)/shard_map/ppermute | solution.py:657
  36.5 1.6 fusion.1
  38.2 0.0 copy-start.7
  38.2 0.0 copy-done.9
  38.2 0.2 fusion.3
  38.4 0.0 copy-done
  38.4 0.2 fusion.7
  38.7 0.0 copy-done.8
  38.8 0.1 copy.26
  38.9 0.8 fusion.4.x_ref
  39.8 123.6 %shard_map.150 = bf16[128,2048]{1,0:T(8,128)(2,1)} custom-call(bf16[128,2176]{1,0:T(8,128)(2,1)} %fusion.4.x_ref, bf16[1,2048,1024]{2,1,0:T(8,128)(2,1)} %wg_hbm.1, bf16[1,2048,1024]{2,1,0:T(8,128)(2,1)} %wu_hbm.1, bf16[1,1024,2048]{2,1,0:T(8,128)(2,1)} %wd_hbm.1), custom_call_target="tpu_custom_call" | custom-call | flops 25769803776 | bytes 12582912 | tf_op jit(solution)/shard_map/pallas_call | solution.py:589
  163.4 0.0 copy-done.7
  163.4 1.9 %copy.28 = bf16[128,2048]{1,0:T(8,128)(2,1)} copy(bf16[128,2048]{1,0:T(8,128)(2,1)} %shard_map.150) | data formatting | bytes 1048576
  (8 shorter events, 0.1 us)
Async XLA Ops:
  0.6 37.8 %copy-start = (bf16[2048,16]{0,1:T(8,128)(2,1)S(1)}, bf16[2048,16]{0,1:T(8,128)(2,1)}, u32[]{:S(2)}) copy-start(bf16[2048,16]{0,1:T(8,128)(2,1)} %param.23) | copy-start | bytes 196612
  1.5 1.0 copy-start.1
  2.6 1.0 copy-start.2
  3.6 1.0 copy-start.3
  4.6 1.0 copy-start.4
  5.7 0.7 copy-start.5
  6.4 0.7 copy-start.6
  33.5 4.7 %copy-start.9 = (f32[2048]{0:T(1024)S(1)}, f32[2048]{0:T(1024)}, u32[]{:S(2)}) copy-start(f32[2048]{0:T(1024)} %param.22) | copy-start | bytes 24580
  33.5 3.0 %collective-permute-start = (f32[128,2048]{1,0:T(8,128)}, f32[128,2048]{1,0:T(8,128)}, u32[]{:S(2)}, u32[]{:S(2)}) collective-permute-start(f32[128,2048]{1,0:T(8,128)} %constant_dynamic-slice_fusion), channel_id=1, source_target_pairs={{0,1},{1,0},{2,3},{3,2},{4,5},{5,4},{6,7},{7,6},{8,9},{9,8},{10,11... | collective-permute-start | bytes 3145736 | tf_op jit(solution)/shard_map/ppermute | solution.py:657
  33.5 5.1 %copy-start.8 = (s32[128,8]{0,1:T(8,128)S(1)}, s32[128,8]{0,1:T(8,128)}, u32[]{:S(2)}) copy-start(s32[128,8]{0,1:T(8,128)} %param.27) | copy-start | bytes 12292
  38.2 125.2 %copy-start.7 = (bf16[128,2048]{1,0:T(8,128)(2,1)}, bf16[128,2048]{1,0:T(8,128)(2,1)S(1)}, u32[]{:S(2)}) copy-start(bf16[128,2048]{1,0:T(8,128)(2,1)S(1)} %get-tuple-element.8) | copy-start | bytes 1572868

commit v5 on v3

--- a/solution.py
+++ b/solution.py
@@ -31,14 +31,19 @@
 def attn_kernel(
     blocks,
     spans,
+    q_hbm,
+    k_hbm,
+    v_hbm,
+    seg_col,
+    seg_row,
+    map_hbm,
+    gain_ref,
+    out_ref,
     q_ref,
     k_ref,
     v_ref,
-    seg_col,
-    seg_row,
     map_ref,
-    gain_ref,
-    out_ref,
+    load_sem,
     key_feat,
     query_feat,
     window,
@@ -58,6 +63,13 @@
     place = lax.axis_index("seq")
     f32, bf16 = jnp.float32, jnp.bfloat16
 
+    sources = ((k_hbm, k_ref), (map_hbm, map_ref), (v_hbm, v_ref), (q_hbm, q_ref))
+    loads = [
+        pltpu.make_async_copy(src, dst, load_sem.at[i]) for i, (src, dst) in enumerate(sources)
+    ]
+    for load in loads:
+        load.start()
+
     barrier = pltpu.get_barrier_semaphore()
     for span in spans:
         for shift in (span, blocks - span):
@@ -126,7 +138,10 @@
         send(0, h)
         return carry
 
+    for load in loads[:3]:
+        load.wait()
     lax.fori_loop(0, heads, key_step, 0)
+    loads[3].wait()
     for i, span in enumerate(spans):
 
         @pl.when(place >= span)
@@ -211,12 +226,19 @@
     count = len(spans)
     dma = pltpu.SemaphoreType.DMA
     f32, bf16 = jnp.float32, jnp.bfloat16
+    in_any = pl.BlockSpec(memory_space=pl.ANY)
+    in_vmem = pl.BlockSpec(memory_space=pltpu.VMEM)
     return pl.pallas_call(
         functools.partial(attn_kernel, blocks, spans),
         out_shape=jax.ShapeDtypeStruct((tokens, heads * dim), bf16),
-        in_specs=[pl.BlockSpec(memory_space=pltpu.VMEM)] * 7,
+        in_specs=[in_any, in_any, in_any, in_vmem, in_vmem, in_any, in_vmem],
         out_specs=pl.BlockSpec(memory_space=pltpu.VMEM),
         scratch_shapes=[
+            pltpu.VMEM(query_proj.shape, bf16),
+            pltpu.VMEM(key_proj.shape, bf16),
+            pltpu.VMEM(value_proj.shape, bf16),
+            pltpu.VMEM(feature_map.shape, bf16),
+            dma((4,)),
             pltpu.VMEM((heads, tokens, feat), bf16),
             pltpu.VMEM((heads, tokens, feat), bf16),
             pltpu.VMEM((heads, feat, dim), f32),
@@ -232,7 +254,7 @@
             dma((count,)),
         ],
         compiler_params=pltpu.CompilerParams(
-            collective_id=1, has_side_effects=True, vmem_limit_bytes=32 * 1024 * 1024
+            collective_id=1, has_side_effects=True, vmem_limit_bytes=VMEM_MOST
         ),
     )(
         query_proj,
@@ -245,7 +267,7 @@
     )
 
 
-TILE = 256
+TILE = 1024
 VMEM_MOST = 63 * 1024 * 1024
 
 

time: 154 us -> 145 us (0.942)
  local copies, waits for them, and re-layouts: 9.44 us -> 4.6 us
  Pallas kernels: 133 us -> 130 us
    unnamed x21 -> x9, local copies, waits for them, and re-layouts: 7.43 us -> 1.91 us
    pallas_call x1, Pallas kernels: 112 us -> 107 us  [moe(): pl.pallas_call(functools.partial(moe_kernel, count, folded, experts), out...]
    pallas_call x1, Pallas kernels: 21.8 us -> 23.5 us  [attention(): pl.pallas_call(functools.partial(attn_kernel, blocks, spans), out_shape=j...]
where the time goes in v5:
time: 145 us
  Pallas kernels  130 us (90%)
  local copies, waits for them, and re-layouts  4.6 us (3%)
  matrix products  3.84 us (3%)
  waiting for transfers between devices  3 us (2%)
  other arithmetic  2.78 us (2%)
    pallas_call x1, Pallas kernels, moe(): pl.pallas_call(functools.partial(moe_kernel, count, folded, experts), out...  107 us
    pallas_call x1, Pallas kernels, attention(): pl.pallas_call(functools.partial(attn_kernel, blocks, spans), out_shape=j...  23.5 us
    dot_general x1, matrix products, shards(): sums = jnp.dot(attn_heads, out_weight, preferred_element_type=jnp.float32)  3.61 us
    ppermute x1, waiting for transfers between devices, shards(): lax.ppermute(lax.dynamic_slice_in_dim(sums, target * row_count, row_count...  3 us
  transfers between devices with their start and end apart: 1, of which 1 were waited for; matrix products, arithmetic and copies ran while one was open for 0% of the time, Pallas kernels for 0%

profile of v5, /device:TPU:0, one launch (start us, length us, event | category | flops | bytes accessed | tf_op | source)
XLA Modules:
  0.0 145.1 jit_solution(1991206419950365536)
XLA Ops:
  0.6 0.0 copy-start
  0.7 1.5 %copy.25.seg_col = s32[256,1]{1,0:T(8,128)} copy(s32[256,1]{0,1:T(1,128)} %bitcast.7) | data formatting | bytes 2048 | tf_op jit(solution)/shard_map/reshape | solution.py:263
  2.2 23.5 %shard_map.149 = bf16[256,1024]{1,0:T(8,128)(2,1)} custom-call(bf16[256,1024]{1,0:T(8,128)(2,1)} %q_hbm.1, bf16[256,1024]{1,0:T(8,128)(2,1)} %k_hbm.1, bf16[256,1024]{1,0:T(8,128)(2,1)} %v_hbm.1, s32[256,1]{1,0:T(8,128)} %copy.25.seg_col, s32[1,256]{1,0:T(1,128)} %bitcast.8, bf16[8,128,256]{2,1,0:T(8,128)(2,1)} %map_hbm.1, f32[1,1024]{1,0:T(1,128)} %bitcast.9), custom_call_target="tpu_custom_call" | custom-call | tf_op jit(solution)/shard_map/pallas_call | solution.py:231
  25.7 3.6 %fusion.6 = f32[256,2048]{1,0:T(8,128)S(1)} fusion(bf16[256,1024]{1,0:T(8,128)(2,1)} %shard_map.149, bf16[1024,2048]{1,0:T(8,128)(2,1)} %param.21), kind=kOutput, calls=%fused_computation.21 | convolution fusion | flops 1073741824 | bytes 6815744 | tf_op jit(solution)/shard_map/dot_general | solution.py:606
  29.3 1.1 constant_dynamic-slice_fusion
  30.4 0.0 copy-start.3
  30.4 0.0 collective-permute-start
  30.4 0.0 copy-start.2
  30.4 3.0 %collective-permute-done = f32[128,2048]{1,0:T(8,128)} collective-permute-done((f32[128,2048]{1,0:T(8,128)}, f32[128,2048]{1,0:T(8,128)}, u32[]{:S(2)}, u32[]{:S(2)}) %collective-permute-start) | collective-permute-done | bytes 1048608 | tf_op jit(solution)/shard_map/ppermute | solution.py:610
  33.4 1.6 %fusion.1 = (f32[128]{0:T(128)S(1)}, bf16[128,2048]{1,0:T(8,128)(2,1)S(1)}) fusion(f32[128,2048]{1,0:T(8,128)} %collective-permute-done, f32[256,2048]{1,0:T(8,128)S(1)} %fusion.6, s32[]{:T(128)S(6)} %select_n.21, bf16[128,2048]{1,0:T(8,128)(2,1)} %param.20), kind=kLoop, calls=%fused_computation.4 | loop fusion | flops 1834880 | bytes 3146244 | tf_op jit(solution)/shard_map/reduce_sum | solution.py:619
  35.0 0.0 copy-start.1
  35.1 0.0 copy-done.3
  35.1 0.2 fusion.3
  35.3 0.0 copy-done
  35.3 0.2 fusion.7
  35.5 0.0 copy-done.2
  35.7 0.1 copy.26
  35.8 0.8 fusion.4.x_ref
  36.6 106.6 %shard_map.150 = bf16[128,2048]{1,0:T(8,128)(2,1)} custom-call(bf16[128,2176]{1,0:T(8,128)(2,1)} %fusion.4.x_ref, bf16[1,2048,1024]{2,1,0:T(8,128)(2,1)} %wg_hbm.1, bf16[1,2048,1024]{2,1,0:T(8,128)(2,1)} %wu_hbm.1, bf16[1,1024,2048]{2,1,0:T(8,128)(2,1)} %wd_hbm.1), custom_call_target="tpu_custom_call" | custom-call | flops 25769803776 | bytes 12582912 | tf_op jit(solution)/shard_map/pallas_call | solution.py:542
  143.2 0.0 copy-done.1
  143.2 1.9 %copy.28 = bf16[128,2048]{1,0:T(8,128)(2,1)} copy(bf16[128,2048]{1,0:T(8,128)(2,1)} %shard_map.150) | data formatting | bytes 1048576
  (7 shorter events, 0.1 us)
Async XLA Ops:
  0.6 34.6 %copy-start = (bf16[2048,16]{0,1:T(8,128)(2,1)S(1)}, bf16[2048,16]{0,1:T(8,128)(2,1)}, u32[]{:S(2)}) copy-start(bf16[2048,16]{0,1:T(8,128)(2,1)} %param.23) | copy-start | bytes 196612
  30.4 4.7 %copy-start.3 = (f32[2048]{0:T(1024)S(1)}, f32[2048]{0:T(1024)}, u32[]{:S(2)}) copy-start(f32[2048]{0:T(1024)} %param.22) | copy-start | bytes 24580
  30.4 3.0 %collective-permute-start = (f32[128,2048]{1,0:T(8,128)}, f32[128,2048]{1,0:T(8,128)}, u32[]{:S(2)}, u32[]{:S(2)}) collective-permute-start(f32[128,2048]{1,0:T(8,128)} %constant_dynamic-slice_fusion), channel_id=1, source_target_pairs={{0,1},{1,0},{2,3},{3,2},{4,5},{5,4},{6,7},{7,6},{8,9},{9,8},{10,11... | collective-permute-start | bytes 3145736 | tf_op jit(solution)/shard_map/ppermute | solution.py:610
  30.4 5.1 %copy-start.2 = (s32[128,8]{0,1:T(8,128)S(1)}, s32[128,8]{0,1:T(8,128)}, u32[]{:S(2)}) copy-start(s32[128,8]{0,1:T(8,128)} %param.27) | copy-start | bytes 12292
  35.0 108.2 %copy-start.1 = (bf16[128,2048]{1,0:T(8,128)(2,1)}, bf16[128,2048]{1,0:T(8,128)(2,1)S(1)}, u32[]{:S(2)}) copy-start(bf16[128,2048]{1,0:T(8,128)(2,1)S(1)} %get-tuple-element.8) | copy-start | bytes 1572868
